TPU v7x, 128 devices: a whole 4x4x4 slice. The times are simulated.
128 devices in a mesh: au: 16 (over x, z_lo, core), ia: 8 (over y, z_hi).
Axes of the slice: x: 4, y: 4, z: 4 (z_hi: 2, z_lo: 2; z = z_hi * 2 + z_lo), core: 2. Of those that a mesh axis runs over, the one named last changes fastest.
Arguments:
- users: float32 [262144, 256], P(('au', 'ia')), may hold values from -6 to 6
- items: float32 [32768, 256], P(('au', 'ia')), may hold values from -6 to 6
- accum: float32 [32768, 256], P(('au', 'ia')), may hold values from 0.1 to 4
- ratings: bfloat16 [16, 8, 2, 16, 128, 128], P('au', 'ia'), may hold values from -6 to 6
- block_users: int32 [16, 8, 2, 16], P(None, 'ia'), may hold values from 0 to 15, as said below
- block_items: int32 [16, 8, 2, 16], P(None, 'ia'), may hold values from 0 to 1, as said below
- block_counts: int32 [16, 8, 2], P(None, 'ia'), may hold values from 2 to 16, as said below
Outputs:
- new_users: float32 [262144, 256], P(('au', 'ia'))
- new_items: float32 [32768, 256], P(('au', 'ia'))
- new_accum: float32 [32768, 256], P(('au', 'ia'))
Inputs may be any that keep to these rules, and one draw needn't show every extreme that they name: In each pair and stratum the 16 slots name distinct (user block, item block) pairs, block_users with block_items. `block_items`: see block_users. Only the first block_counts slots of a pair and stratum are observed; in every stratum some pair has all 16 slots observed.
All inputs are finite; a program needn't handle non-finite values.
Results may differ from a plain program's by a relative error of at most 0.008.
Values may be sent and summed in bfloat16 or wider, within the bound.
No kernel may reach another device: no remote copies, remote signals or barrier semaphores. Data moves between devices by JAX's collectives and lax.ppermute only.
A program may use at most 64 MiB of HBM per device.

v0:
```python
import math

import jax
import jax.numpy as jnp
from jax import lax
from jax.sharding import PartitionSpec as P

STEPS = 2


rate_users = 0.1
rate_items = 0.1
weight_decay = 0.02
adagrad_eps = 1e-08


def shifted(value, axis, steps):
    count = lax.axis_size(axis)
    pairs = [(source, (source + steps) % count) for source in range(count)]
    return lax.ppermute(value, axis, pairs)


def select_sum(form, pick_table, part_values):
    high_half = part_values.astype(jnp.bfloat16)
    low_half = (part_values - high_half.astype(jnp.float32)).astype(jnp.bfloat16)
    total = jnp.einsum(form, pick_table, high_half, preferred_element_type=jnp.float32)
    return total + jnp.einsum(form, pick_table, low_half, preferred_element_type=jnp.float32)


def block_sums(user_copy, item_copy, rating_set, user_ids, item_ids, live_count, width):
    inv_root = 1.0 / math.sqrt(user_copy.shape[-1])
    user_rows = user_copy[user_ids]
    item_rows = item_copy[item_ids]
    predicted = jnp.einsum("nrk,nck->nrc", user_rows, item_rows, preferred_element_type=jnp.float32)
    slot_ids = jnp.arange(width, dtype=jnp.int32)
    live_mask = (slot_ids < live_count)[:, None, None]
    residual = jnp.where(
        live_mask, rating_set.astype(jnp.float32) - inv_root * predicted, 0.0
    ).astype(jnp.bfloat16)
    user_part = jnp.einsum("nrc,nck->nrk", residual, item_rows, preferred_element_type=jnp.float32)
    item_part = jnp.einsum("nrc,nrk->nck", residual, user_rows, preferred_element_type=jnp.float32)
    pick_users = (
        user_ids[:, None] == jnp.arange(user_copy.shape[0], dtype=jnp.int32)[None, :]
    ).astype(jnp.bfloat16)
    pick_items = (
        item_ids[:, None] == jnp.arange(item_copy.shape[0], dtype=jnp.int32)[None, :]
    ).astype(jnp.bfloat16)
    user_sum = select_sum("nu,nrk->urk", pick_users, user_part)
    item_sum = select_sum("ni,nck->ick", pick_items, item_part)
    return (user_sum, item_sum)


def stratum_update(user_slab, item_slab, accum_slab, rating_set, user_ids, item_ids, live_count):
    inv_root = 1.0 / math.sqrt(user_slab.shape[-1])
    slot_total = rating_set.shape[0]
    for repeat in range(STEPS):
        user_copy = user_slab.astype(jnp.bfloat16)
        item_copy = item_slab.astype(jnp.bfloat16)
        user_sum, item_sum = block_sums(
            user_copy, item_copy, rating_set, user_ids, item_ids, live_count, slot_total
        )
        user_grad = weight_decay * user_slab - inv_root * user_sum
        item_grad = weight_decay * item_slab - inv_root * item_sum
        user_slab = user_slab - rate_users * user_grad
        accum_slab = accum_slab + item_grad * item_grad
        item_slab = item_slab - rate_items * item_grad / jnp.sqrt(accum_slab + adagrad_eps)
    return (user_slab, item_slab, accum_slab)


def pick_row(table, position):
    return lax.dynamic_index_in_dim(table, position, 0, keepdims=False)


def local(users, items, accum, ratings, block_users, block_items, block_counts):
    rank_width = users.shape[-1]
    block_size = ratings.shape[-1]
    user_slab = users.reshape(-1, block_size, rank_width)
    item_slab = items.reshape(-1, block_size, rank_width)
    accum_slab = accum.reshape(-1, block_size, rank_width)
    rating_all = ratings[0, 0]
    user_lists = block_users[:, 0]
    item_lists = block_items[:, 0]
    count_lists = block_counts[:, 0]
    strata_count = rating_all.shape[0]
    position = lax.axis_index("au")
    for stratum in range(strata_count):
        if stratum > 0:
            user_slab = shifted(user_slab, "au", 1)
            item_slab, accum_slab = shifted((item_slab, accum_slab), "ia", 1)
        user_slab, item_slab, accum_slab = stratum_update(
            user_slab,
            item_slab,
            accum_slab,
            rating_all[stratum],
            pick_row(user_lists[:, stratum], position),
            pick_row(item_lists[:, stratum], position),
            pick_row(count_lists[:, stratum], position),
        )
    user_slab = shifted(user_slab, "au", 1 - strata_count)
    item_slab, accum_slab = shifted((item_slab, accum_slab), "ia", 1 - strata_count)
    return (
        user_slab.reshape(users.shape),
        item_slab.reshape(items.shape),
        accum_slab.reshape(accum.shape),
    )


def solution(mesh):
    return jax.shard_map(
        local,
        mesh=mesh,
        in_specs=(
            P(("au", "ia"), None),
            P(("au", "ia"), None),
            P(("au", "ia"), None),
            P("au", "ia", None, None, None, None),
            P(None, "ia", None, None),
            P(None, "ia", None, None),
            P(None, "ia", None),
        ),
        out_specs=(P(("au", "ia"), None), P(("au", "ia"), None), P(("au", "ia"), None)),
        check_vma=False,
    )
```

profile of v0, /device:TPU:0, one launch (start us, length us, event | category | flops | bytes accessed | tf_op | source)
XLA Modules:
  0.0 135.4 jit_solution(13984208856220734847)
XLA Ops:
  0.6 1.4 %fusion.93 = (s32[16,1,16]{2,1,0:T(1,128)}, s32[16,1,16]{2,1,0:T(1,128)S(1)}) fusion(s32[16,2,16]{2,1,0:T(2,128)} %bitcast.111), kind=kLoop, calls=%fused_computation.141 | loop fusion | bytes 4096 | tf_op jit(solution)/shard_map/slice | solution.py:95
  2.0 0.8 fusion.92
  2.9 1.3 fusion.94
  5.5 1.0 convert_element_type.133
  6.4 1.7 %convert_element_type.132 = bf16[16,128,256]{2,1,0:T(8,128)(2,1)S(1)} convert(f32[16,128,256]{2,1,0:T(8,128)} %bitcast.101) | non-fusion elementwise | flops 524288 | bytes 3145728 | tf_op jit(solution)/shard_map/convert_element_type | solution.py:57
  9.4 1.5 %fusion.11 = bf16[16,128,128]{2,1,0:T(8,128)(2,1)S(1)} fusion(bf16[16,128,256]{2,1,0:T(8,128)(2,1)S(1)} %gather_fusion, bf16[16,128,256]{2,1,0:T(8,128)(2,1)S(1)} %gather_fusion.1, pred[16]{0:T(512)(128)(4,1)S(1)} %iota_compare_fusion.13, bf16[1,1,2,16,128,128]{5,4,3,2,1,0:T(8,128)(2,1)} %param.10), kind=kOutput, calls=%fused_computation.35 | convolution fusion | flops 135528448 | bytes 3145744 | tf_op jit(solution)/shard_map/nrk,nck->nrc/dot_general | solution.py:34
  11.4 1.4 %subtract_convert_fusion.7 = (bf16[16,128,256]{2,1,0:T(8,128)(2,1)S(1)}, bf16[16,128,256]{2,1,0:T(8,128)(2,1)}) fusion(bf16[16,128,128]{2,1,0:T(8,128)(2,1)S(1)} %fusion.11, bf16[16,128,256]{2,1,0:T(8,128)(2,1)S(1)} %gather_fusion.1), kind=kOutput, calls=%fused_computation.19 | convolution fusion | flops 136314880 | bytes 3670016 | tf_op jit(solution)/shard_map/nrc,nck->nrk/dot_general | solution.py:40
  12.8 0.7 fusion.33
  14.2 0.8 fusion.91
  15.0 1.7 %gather_fusion.3 = bf16[16,128,256]{2,1,0:T(8,128)(2,1)} fusion(bf16[2,128,256]{2,1,0:T(8,128)(2,1)S(1)} %get-tuple-element.21, s32[1024]{0:T(1024)} %copy-done.22), kind=kCustom, calls=%fused_computation.3 | custom fusion | bytes 2097216 | tf_op jit(solution)/shard_map/gather | solution.py:33
  16.8 0.7 fusion.38
  17.5 0.9 copy-done
  18.3 2.1 %fusion.95 = (bf16[16,128,256]{2,0,1:T(8,128)(2,1)S(1)}, f32[16,128,256]{2,0,1:T(8,128)S(1)}) fusion(f32[16,128,256]{2,0,1:T(8,128)S(1)} %fusion.38, bf16[16,128,256]{2,1,0:T(8,128)(2,1)S(1)} %get-tuple-element.25, s32[16]{0:T(128)S(1)} %get-tuple-element.39, f32[16,128,256]{2,1,0:T(8,128)S(1)} %bitcast.102), kind=kOutput, calls=%fused_computation.143 | convolution fusion | flops 20447488 | bytes 8388672 | tf_op jit(solution)/shard_map/nu,nrk->urk/dot_general | solution.py:27
  20.4 1.3 copy.84
  21.7 2.0 %gather_fusion.2 = bf16[16,128,256]{2,1,0:T(8,128)(2,1)S(1)} fusion(bf16[16,128,256]{2,1,0:T(8,128)(2,1)} %copy.84, s32[1024]{0:T(1024)} %copy-done.21), kind=kCustom, calls=%fused_computation.2 | custom fusion | bytes 2097216 | tf_op jit(solution)/shard_map/gather | solution.py:32
  23.7 1.9 %fusion.10 = bf16[16,128,128]{2,1,0:T(8,128)(2,1)S(1)} fusion(bf16[16,128,256]{2,1,0:T(8,128)(2,1)S(1)} %gather_fusion.2, bf16[16,128,256]{2,1,0:T(8,128)(2,1)} %gather_fusion.3, pred[16]{0:T(512)(128)(4,1)S(1)} %copy-done.27, bf16[1,1,2,16,128,128]{5,4,3,2,1,0:T(8,128)(2,1)} %param.10), kind=kOutput, calls=%fused_computation.34 | convolution fusion | flops 135528448 | bytes 3145744 | tf_op jit(solution)/shard_map/nrk,nck->nrc/dot_general | solution.py:34
  26.1 0.7 fusion.31
  26.8 2.4 %multiply_subtract_fusion.2 = f32[16,128,256]{2,0,1:T(8,128)} fusion(f32[16,128,256]{2,0,1:T(8,128)S(1)} %get-tuple-element.34, f32[16,128,256]{2,0,1:T(8,128)S(1)} %fusion.31, bf16[16,128,256]{2,1,0:T(8,128)(2,1)S(1)} %get-tuple-element.19, s32[16]{0:T(128)S(1)} %get-tuple-element.39), kind=kOutput, calls=%fused_computation.15 | convolution fusion | flops 19923200 | bytes 7340096 | tf_op jit(solution)/shard_map/nu,nrk->urk/dot_general | solution.py:27
  29.7 0.7 fusion.26
  31.1 0.9 multiply_subtract_fusion.6
  31.9 4.0 %collective-permute-start.1 = (f32[2,128,256]{2,1,0:T(8,128)S(1)}, f32[2,128,256]{2,1,0:T(8,128)S(1)}, u32[]{:S(2)}, u32[]{:S(2)}) collective-permute-start(f32[2,128,256]{2,1,0:T(8,128)S(1)} %get-tuple-element.15), channel_id=1, source_target_pairs={{0,1},{1,2},{2,3},{3,4},{4,5},{5,6},{6,7},{7,0},{8,9},{9,10},{10,1... | collective-permute-start | bytes 786440 | tf_op jit(solution)/shard_map/ppermute | solution.py:20
  39.0 5.6 %collective-permute-done.1 = f32[2,128,256]{2,1,0:T(8,128)S(1)} collective-permute-done((f32[2,128,256]{2,1,0:T(8,128)S(1)}, f32[2,128,256]{2,1,0:T(8,128)S(1)}, u32[]{:S(2)}, u32[]{:S(2)}) %collective-permute-start.1) | collective-permute-done | bytes 262176 | tf_op jit(solution)/shard_map/ppermute | solution.py:20
  44.5 0.7 copy-done.14
  45.9 11.1 %collective-permute-done = f32[16,128,256]{2,0,1:T(8,128)S(1)} collective-permute-done((f32[16,128,256]{2,0,1:T(8,128)}, f32[16,128,256]{2,0,1:T(8,128)S(1)}, u32[]{:S(2)}, u32[]{:S(2)}) %collective-permute-start) | collective-permute-done | bytes 2097184 | tf_op jit(solution)/shard_map/ppermute | solution.py:20
  57.2 1.3 copy.92
  58.5 2.8 %gather_fusion.4 = bf16[16,128,256]{2,1,0:T(8,128)(2,1)} fusion(bf16[16,128,256]{2,1,0:T(8,128)(2,1)} %copy.92, s32[1024]{0:T(1024)S(1)} %pad_clamp_fusion.1), kind=kCustom, calls=%fused_computation.4 | custom fusion | bytes 2097216 | tf_op jit(solution)/shard_map/gather | solution.py:32
  61.3 1.9 %fusion.9 = bf16[16,128,128]{2,1,0:T(8,128)(2,1)S(1)} fusion(bf16[16,128,256]{2,1,0:T(8,128)(2,1)} %gather_fusion.4, bf16[16,128,256]{2,1,0:T(8,128)(2,1)S(1)} %gather_fusion.5, pred[16]{0:T(512)(128)(4,1)S(1)} %iota_compare_fusion.12, bf16[1,1,2,16,128,128]{5,4,3,2,1,0:T(8,128)(2,1)} %param.10), kind=kOutput, calls=%fused_computation.33 | convolution fusion | flops 135528448 | bytes 3145744 | tf_op jit(solution)/shard_map/nrk,nck->nrc/dot_general | solution.py:34
  63.7 0.7 copy-done.5
  64.4 1.4 %subtract_convert_fusion.3 = (bf16[16,128,256]{2,1,0:T(8,128)(2,1)S(1)}, bf16[16,128,256]{2,1,0:T(8,128)(2,1)}) fusion(bf16[16,128,128]{2,1,0:T(8,128)(2,1)S(1)} %fusion.9, bf16[16,128,256]{2,1,0:T(8,128)(2,1)S(1)} %copy-done.5), kind=kOutput, calls=%fused_computation.13 | convolution fusion | flops 136314880 | bytes 3670016 | tf_op jit(solution)/shard_map/nrc,nck->nrk/dot_general | solution.py:40
  66.5 0.7 fusion.21
  67.2 0.7 copy-done.8
  67.9 1.8 %fusion.90 = (bf16[2,128,256]{2,1,0:T(8,128)(2,1)S(1)}, f32[2,128,256]{2,1,0:T(8,128)}) fusion(f32[2,128,256]{2,1,0:T(8,128)S(1)} %copy-done.15, f32[2,128,256]{2,1,0:T(8,128)} %collective-permute-done.2, f32[2,128,256]{2,0,1:T(2,128)S(1)} %fusion.19, f32[2,128,256]{2,0,1:T(2,128)S(1)} %fusion.21), kind=kLoop, calls=%fused_computation.138 | loop fusion | flops 720896 | bytes 1441792 | tf_op jit(solution)/shard_map/convert_element_type | solution.py:58
  69.6 1.6 %gather_fusion.7 = bf16[16,128,256]{2,1,0:T(8,128)(2,1)} fusion(bf16[2,128,256]{2,1,0:T(8,128)(2,1)S(1)} %get-tuple-element.9, s32[1024]{0:T(1024)S(1)} %pad_clamp_fusion), kind=kCustom, calls=%fused_computation.7 | custom fusion | bytes 2097216 | tf_op jit(solution)/shard_map/gather | solution.py:33
  71.3 1.9 %fusion.24 = f32[16,128,256]{2,0,1:T(8,128)S(1)} fusion(bf16[16,128,256]{2,1,0:T(8,128)(2,1)} %get-tuple-element.14, s32[16]{0:T(128)S(1)} %fusion.88), kind=kOutput, calls=%fused_computation.48 | convolution fusion | flops 16777472 | bytes 3145792 | tf_op jit(solution)/shard_map/nu,nrk->urk/dot_general | solution.py:26
  73.2 2.4 %fusion.96 = (bf16[16,128,256]{2,0,1:T(8,128)(2,1)S(1)}, f32[16,128,256]{2,0,1:T(8,128)}) fusion(f32[16,128,256]{2,0,1:T(8,128)S(1)} %collective-permute-done, f32[16,128,256]{2,0,1:T(8,128)S(1)} %fusion.24, bf16[16,128,256]{2,1,0:T(8,128)(2,1)S(1)} %get-tuple-element.13, s32[16]{0:T(128)S(1)} %fusion.88), kind=kOutput, calls=%fused_computation.144 | convolution fusion | flops 20447488 | bytes 8388672 | tf_op jit(solution)/shard_map/nu,nrk->urk/dot_general | solution.py:27
  76.8 1.5 %fusion.8 = bf16[16,128,128]{2,1,0:T(8,128)(2,1)S(1)} fusion(bf16[16,128,256]{2,1,0:T(8,128)(2,1)S(1)} %gather_fusion.6, bf16[16,128,256]{2,1,0:T(8,128)(2,1)S(1)} %copy-done.3, pred[16]{0:T(512)(128)(4,1)S(1)} %copy-done.25, bf16[1,1,2,16,128,128]{5,4,3,2,1,0:T(8,128)(2,1)} %param.10), kind=kOutput, calls=%fused_computation.32 | convolution fusion | flops 135528448 | bytes 3145744 | tf_op jit(solution)/shard_map/nrk,nck->nrc/dot_general | solution.py:34
  78.7 0.7 fusion.17
  79.5 0.9 copy-done.1
  80.3 1.0 multiply_subtract_fusion
  81.3 7.3 %collective-permute-start.3 = (f32[16,128,256]{2,0,1:T(8,128)S(1)}, f32[16,128,256]{2,0,1:T(8,128)S(1)}, u32[]{:S(2)}, u32[]{:S(2)}) collective-permute-start(f32[16,128,256]{2,0,1:T(8,128)S(1)} %multiply_subtract_fusion), channel_id=1, source_target_pairs={{0,120},{8,0},{16,8},{24,16},{32,24},{40,32},{48,40},{56,48},{64,5... | collective-permute-start | bytes 6291464 | tf_op jit(solution)/shard_map/ppermute | solution.py:20
  89.1 0.7 fusion.12
  90.5 1.1 multiply_subtract_fusion.4
  91.6 10.5 %collective-permute-start.4 = (f32[2,128,256]{2,1,0:T(8,128)S(1)}, f32[2,128,256]{2,1,0:T(8,128)S(1)}, u32[]{:S(2)}, u32[]{:S(2)}) collective-permute-start(f32[2,128,256]{2,1,0:T(8,128)S(1)} %get-tuple-element.3), channel_id=1, source_target_pairs={{0,7},{1,0},{2,1},{3,2},{4,3},{5,4},{6,5},{7,6},{8,15},{9,8},{10,9... | collective-permute-start | bytes 786440 | tf_op jit(solution)/shard_map/ppermute | solution.py:20
  102.1 23.7 %collective-permute-done.4 = f32[2,128,256]{2,1,0:T(8,128)S(1)} collective-permute-done((f32[2,128,256]{2,1,0:T(8,128)S(1)}, f32[2,128,256]{2,1,0:T(8,128)S(1)}, u32[]{:S(2)}, u32[]{:S(2)}) %collective-permute-start.4) | collective-permute-done | bytes 262176 | tf_op jit(solution)/shard_map/ppermute | solution.py:20
  125.9 5.6 %collective-permute-done.5 = f32[2,128,256]{2,1,0:T(8,128)S(1)} collective-permute-done((f32[2,128,256]{2,1,0:T(8,128)S(1)}, f32[2,128,256]{2,1,0:T(8,128)S(1)}, u32[]{:S(2)}, u32[]{:S(2)}) %collective-permute-start.5) | collective-permute-done | bytes 262176 | tf_op jit(solution)/shard_map/ppermute | solution.py:20
  131.5 2.5 %copy.108 = f32[16,128,256]{2,1,0:T(8,128)} copy(f32[16,128,256]{2,0,1:T(8,128)S(1)} %collective-permute-done.3) | data formatting | bytes 4194304 | tf_op jit(solution)/shard_map/ppermute | solution.py:20
  134.0 0.7 copy.225
  134.7 0.7 copy.226
  (87 shorter events, 13.2 us)
Async XLA Ops:
  5.4 4.0 %copy-start.26 = (pred[16]{0:T(512)(128)(4,1)}, pred[16]{0:T(512)(128)(4,1)S(1)}, u32[]{:S(2)}) copy-start(pred[16]{0:T(512)(128)(4,1)S(1)} %iota_compare_fusion.13) | copy-start | bytes 52
  5.4 3.4 %copy-start.21 = (s32[1024]{0:T(1024)}, s32[1024]{0:T(1024)S(1)}, u32[]{:S(2)}) copy-start(s32[1024]{0:T(1024)S(1)} %pad_clamp_fusion.3) | copy-start | bytes 12292
  5.5 3.3 %copy-start.22 = (s32[1024]{0:T(1024)}, s32[1024]{0:T(1024)S(1)}, u32[]{:S(2)}) copy-start(s32[1024]{0:T(1024)S(1)} %pad_clamp_fusion.2) | copy-start | bytes 12292
  12.8 1.4 %copy-start.12 = (f32[256,256]{1,0:T(8,128)S(1)}, f32[256,256]{1,0:T(8,128)}, u32[]{:S(2)}) copy-start(f32[256,256]{1,0:T(8,128)} %param.8) | copy-start | bytes 786436
  12.8 1.4 %copy-start.17 = (f32[256,256]{1,0:T(8,128)S(1)}, f32[256,256]{1,0:T(8,128)}, u32[]{:S(2)}) copy-start(f32[256,256]{1,0:T(8,128)} %param.9) | copy-start | bytes 786436
  14.2 3.3 %copy-start.10 = (f32[2,128,256]{2,0,1:T(2,128)}, f32[2,128,256]{2,0,1:T(2,128)S(1)}, u32[]{:S(2)}) copy-start(f32[2,128,256]{2,0,1:T(2,128)S(1)} %fusion.35) | copy-start | bytes 786436
  14.2 2.6 %copy-start.7 = (bf16[16,128,256]{2,1,0:T(8,128)(2,1)S(1)}, bf16[16,128,256]{2,1,0:T(8,128)(2,1)}, u32[]{:S(2)}) copy-start(bf16[16,128,256]{2,1,0:T(8,128)(2,1)} %get-tuple-element.26) | copy-start | bytes 3145732
  16.7 1.6 %copy-start = (f32[2048,256]{1,0:T(8,128)S(1)}, f32[2048,256]{1,0:T(8,128)}, u32[]{:S(2)}) copy-start(f32[2048,256]{1,0:T(8,128)} %param.7) | copy-start | bytes 6291460
  20.4 3.3 %copy-start.27 = (pred[16]{0:T(512)(128)(4,1)S(1)}, pred[16]{0:T(512)(128)(4,1)}, u32[]{:S(2)}) copy-start(pred[16]{0:T(512)(128)(4,1)} %copy-done.26) | copy-start | bytes 52
  23.7 1.9 %copy-start.2 = (bf16[16,128,256]{2,1,0:T(8,128)(2,1)S(1)}, bf16[16,128,256]{2,1,0:T(8,128)(2,1)}, u32[]{:S(2)}) copy-start(bf16[16,128,256]{2,1,0:T(8,128)(2,1)} %gather_fusion.3) | copy-start | bytes 3145732
  29.1 27.9 %collective-permute-start = (f32[16,128,256]{2,0,1:T(8,128)}, f32[16,128,256]{2,0,1:T(8,128)S(1)}, u32[]{:S(2)}, u32[]{:S(2)}) collective-permute-start(f32[16,128,256]{2,0,1:T(8,128)} %multiply_subtract_fusion.2), channel_id=1, source_target_pairs={{0,8},{8,16},{16,24},{24,32},{32,40},{40,48},{48,56},{56,64},{64,7... | collective-permute-start | bytes 6291464 | tf_op jit(solution)/shard_map/ppermute | solution.py:20
  29.6 1.4 %copy-start.11 = (f32[2,128,256]{2,0,1:T(2,128)S(1)}, f32[2,128,256]{2,0,1:T(2,128)}, u32[]{:S(2)}) copy-start(f32[2,128,256]{2,0,1:T(2,128)} %copy-done.10) | copy-start | bytes 786436
  29.6 1.4 %copy-start.13 = (f32[256,256]{1,0:T(8,128)S(1)}, f32[256,256]{1,0:T(8,128)}, u32[]{:S(2)}) copy-start(f32[256,256]{1,0:T(8,128)} %param.8) | copy-start | bytes 786436
  29.7 1.4 %copy-start.18 = (f32[256,256]{1,0:T(8,128)S(1)}, f32[256,256]{1,0:T(8,128)}, u32[]{:S(2)}) copy-start(f32[256,256]{1,0:T(8,128)} %param.9) | copy-start | bytes 786436
  29.7 1.4 %copy-start.20 = (f32[2,128,256]{2,1,0:T(8,128)S(1)}, f32[2,128,256]{2,1,0:T(8,128)}, u32[]{:S(2)}) copy-start(f32[2,128,256]{2,1,0:T(8,128)} %get-tuple-element.22) | copy-start | bytes 786436
  30.4 6.2 %copy-start.23 = (s32[16,1]{0,1:T(1,128)S(1)}, s32[16,1]{0,1:T(1,128)}, u32[]{:S(2)}) copy-start(s32[16,1]{0,1:T(1,128)} %get-tuple-element.31) | copy-start | bytes 196
  31.9 12.6 %collective-permute-start.1 = (f32[2,128,256]{2,1,0:T(8,128)S(1)}, f32[2,128,256]{2,1,0:T(8,128)S(1)}, u32[]{:S(2)}, u32[]{:S(2)}) collective-permute-start(f32[2,128,256]{2,1,0:T(8,128)S(1)} %get-tuple-element.15), channel_id=1, source_target_pairs={{0,1},{1,2},{2,3},{3,4},{4,5},{5,6},{6,7},{7,0},{8,9},{9,10},{10,1... | collective-permute-start | bytes 786440 | tf_op jit(solution)/shard_map/ppermute | solution.py:20
  35.9 31.3 %collective-permute-start.2 = (f32[2,128,256]{2,1,0:T(8,128)}, f32[2,128,256]{2,1,0:T(8,128)}, u32[]{:S(2)}, u32[]{:S(2)}) collective-permute-start(f32[2,128,256]{2,1,0:T(8,128)} %get-tuple-element.16), channel_id=1, source_target_pairs={{0,1},{1,2},{2,3},{3,4},{4,5},{5,6},{6,7},{7,0},{8,9},{9,10},{10,1... | collective-permute-start | bytes 786440 | tf_op jit(solution)/shard_map/ppermute | solution.py:20
  38.9 22.4 %copy-start.24 = (pred[16]{0:T(512)(128)(4,1)}, pred[16]{0:T(512)(128)(4,1)S(1)}, u32[]{:S(2)}) copy-start(pred[16]{0:T(512)(128)(4,1)S(1)} %iota_compare_fusion.12) | copy-start | bytes 52
  44.5 0.7 copy-start.14
  45.9 15.4 %copy-start.4 = (bf16[16,128,256]{2,1,0:T(8,128)(2,1)}, bf16[16,128,256]{2,1,0:T(8,128)(2,1)S(1)}, u32[]{:S(2)}) copy-start(bf16[16,128,256]{2,1,0:T(8,128)(2,1)S(1)} %gather_fusion.5) | copy-start | bytes 3145732
  61.3 1.9 %copy-start.6 = (bf16[16,128,256]{2,1,0:T(8,128)(2,1)S(1)}, bf16[16,128,256]{2,1,0:T(8,128)(2,1)}, u32[]{:S(2)}) copy-start(bf16[16,128,256]{2,1,0:T(8,128)(2,1)} %gather_fusion.4) | copy-start | bytes 3145732
  63.2 1.2 copy-start.5
  65.8 2.1 %copy-start.15 = (f32[2,128,256]{2,1,0:T(8,128)S(1)}, f32[2,128,256]{2,1,0:T(8,128)}, u32[]{:S(2)}) copy-start(f32[2,128,256]{2,1,0:T(8,128)} %copy-done.14) | copy-start | bytes 786436
  67.2 0.7 copy-start.8
  75.6 1.2 copy-start.3
  75.6 1.2 copy-start.25
  78.7 1.6 %copy-start.1 = (f32[16,128,256]{2,0,1:T(8,128)S(1)}, f32[16,128,256]{2,0,1:T(8,128)}, u32[]{:S(2)}) copy-start(f32[16,128,256]{2,0,1:T(8,128)} %get-tuple-element.36) | copy-start | bytes 6291460
  81.3 50.2 %collective-permute-start.3 = (f32[16,128,256]{2,0,1:T(8,128)S(1)}, f32[16,128,256]{2,0,1:T(8,128)S(1)}, u32[]{:S(2)}, u32[]{:S(2)}) collective-permute-start(f32[16,128,256]{2,0,1:T(8,128)S(1)} %multiply_subtract_fusion), channel_id=1, source_target_pairs={{0,120},{8,0},{16,8},{24,16},{32,24},{40,32},{48,40},{56,48},{64,5... | collective-permute-start | bytes 6291464 | tf_op jit(solution)/shard_map/ppermute | solution.py:20
  89.1 1.4 %copy-start.9 = (f32[2,128,256]{2,0,1:T(2,128)S(1)}, f32[2,128,256]{2,0,1:T(2,128)}, u32[]{:S(2)}) copy-start(f32[2,128,256]{2,0,1:T(2,128)} %copy-done.8) | copy-start | bytes 786436
  89.1 1.4 %copy-start.16 = (f32[2,128,256]{2,1,0:T(8,128)S(1)}, f32[2,128,256]{2,1,0:T(8,128)}, u32[]{:S(2)}) copy-start(f32[2,128,256]{2,1,0:T(8,128)} %copy-done.14) | copy-start | bytes 786436
  89.1 1.4 %copy-start.19 = (f32[2,128,256]{2,1,0:T(8,128)S(1)}, f32[2,128,256]{2,1,0:T(8,128)}, u32[]{:S(2)}) copy-start(f32[2,128,256]{2,1,0:T(8,128)} %get-tuple-element.10) | copy-start | bytes 786436
  91.6 34.3 %collective-permute-start.4 = (f32[2,128,256]{2,1,0:T(8,128)S(1)}, f32[2,128,256]{2,1,0:T(8,128)S(1)}, u32[]{:S(2)}, u32[]{:S(2)}) collective-permute-start(f32[2,128,256]{2,1,0:T(8,128)S(1)} %get-tuple-element.3), channel_id=1, source_target_pairs={{0,7},{1,0},{2,1},{3,2},{4,3},{5,4},{6,5},{7,6},{8,15},{9,8},{10,9... | collective-permute-start | bytes 786440 | tf_op jit(solution)/shard_map/ppermute | solution.py:20
  102.0 29.4 %collective-permute-start.5 = (f32[2,128,256]{2,1,0:T(8,128)S(1)}, f32[2,128,256]{2,1,0:T(8,128)S(1)}, u32[]{:S(2)}, u32[]{:S(2)}) collective-permute-start(f32[2,128,256]{2,1,0:T(8,128)S(1)} %get-tuple-element.4), channel_id=1, source_target_pairs={{0,7},{1,0},{2,1},{3,2},{4,3},{5,4},{6,5},{7,6},{8,15},{9,8},{10,9... | collective-permute-start | bytes 786440 | tf_op jit(solution)/shard_map/ppermute | solution.py:20
where the time goes:
time: 137 us; the launch traced here: 135 us
  waiting for transfers between devices  46 us (34%)
  matrix products  29.6 us (22%)
  local copies, waits for them, and re-layouts  27 us (20%)
  starting transfers between devices  22.5 us (16%)
  other arithmetic  9.28 us (7%)
    ppermute x6, waiting for transfers between devices, shifted(): return lax.ppermute(value, axis, pairs)  46 us
    ppermute x6, starting transfers between devices, shifted(): return lax.ppermute(value, axis, pairs)  22.5 us
    dot_general x8, matrix products, select_sum(): jnp.einsum(form, pick_table, low_half, preferred_element_type=jnp.float32)  10.5 us
    dot_general x8, matrix products, select_sum(): jnp.einsum(form, pick_table, high_half, preferred_element_type=jnp.float32)  6.77 us
    dot_general x4, matrix products, block_sums(): jnp.einsum('nrk,nck->nrc', user_rows, item_rows, preferred_element_type=j...  6.73 us
    gather x4, local copies, waits for them, and re-layouts, block_sums(): user_rows = user_copy[user_ids]  6.01 us
    unnamed x58, local copies, waits for them, and re-layouts  5.62 us
    gather x4, local copies, waits for them, and re-layouts, block_sums(): item_rows = item_copy[item_ids]  4.58 us
  transfers between devices with their start and end apart: 6, of which 4 were waited for; matrix products, arithmetic and copies ran while one was open for 13% of the time, Pallas kernels for 0%

commit v1 on v0

v1 whole, which is shorter than its diff:
```python
import functools
import math

import jax
import jax.numpy as jnp
from jax import lax
from jax.experimental import pallas as pl
from jax.experimental.pallas import tpu as pltpu
from jax.sharding import PartitionSpec as P

STEPS = 2

rate_users = 0.1
rate_items = 0.1
weight_decay = 0.02
adagrad_eps = 1e-08

CHUNK = 256
F32 = jnp.float32
BF16 = jnp.bfloat16


def dot_nt(left, right):
    return lax.dot_general(left, right, (((1,), (1,)), ((), ())), preferred_element_type=F32)


def dot_nn(left, right):
    return lax.dot_general(left, right, (((1,), (0,)), ((), ())), preferred_element_type=F32)


def dot_tn(left, right):
    return lax.dot_general(left, right, (((0,), (0,)), ((), ())), preferred_element_type=F32)


def rating_copies(source, dense, ids_u, ids_i, row, stratum, sems, block):
    copies = []
    for n in range(source.shape[0]):
        user_at = pl.multiple_of(ids_u[row, 0, stratum, n] * block, block)
        item_at = pl.multiple_of(ids_i[row, 0, stratum, n] * block, block)
        copies.append(
            pltpu.make_async_copy(
                source.at[n], dense.at[pl.ds(user_at, block), pl.ds(item_at, block)], sems.at[n]
            )
        )
    return copies


def mark_live(live, ids_u, ids_i, counts, row, stratum, item_blocks):
    for at in range(live.shape[0]):
        live[at] = 0
    for n in range(ids_u.shape[-1]):
        @pl.when(n < counts[0, stratum, row])
        def _():
            live[ids_u[row, 0, stratum, n] * item_blocks + ids_i[row, 0, stratum, n]] = 1


def residual_chunk(predicted, dense, live, first, block, inv_root, out):
    rows, cols = predicted.shape
    item_blocks = cols // block
    for r in range(rows // block):
        for c in range(item_blocks):
            at = (pl.ds(first + r * block, block), pl.ds(c * block, block))
            part = predicted[r * block : (r + 1) * block, c * block : (c + 1) * block]
            flag = live[(first // block + r) * item_blocks + c] != 0
            value = jnp.where(flag, dense[at].astype(F32) - inv_root * part, 0.0)
            out[at] = value.astype(BF16)


def user_step(user, total, inv_root):
    return user - rate_users * (weight_decay * user - inv_root * total)


def item_step(item, acc, total, inv_root):
    grad = weight_decay * item - inv_root * total
    acc = acc + grad * grad
    return item - rate_items * grad / jnp.sqrt(acc + adagrad_eps), acc


def stratum_body(user, item, acc, dense, live, resid, item_total, user_out, copy_out, block):
    rows, width = user.shape
    inv_root = 1.0 / math.sqrt(width)
    for step in range(STEPS):
        last = step == STEPS - 1
        item_copy = item.astype(BF16)
        if last:
            copy_out[...] = item_copy
        source = user if step == 0 else user_out
        for c in range(rows // CHUNK):
            span = pl.ds(c * CHUNK, CHUNK)
            user_now = source[span, :]
            user_copy = user_now.astype(BF16)
            predicted = dot_nt(user_copy, item_copy)
            residual_chunk(predicted, dense, live, c * CHUNK, block, inv_root, resid)
            here = resid[span, :]
            part = dot_tn(here, user_copy)
            item_total[...] = part if c == 0 else item_total[...] + part
            if not last:
                user_out[span, :] = user_step(user_now, dot_nn(here, item_copy), inv_root)
        item, acc = item_step(item, acc, item_total[...], inv_root)
    return item, acc


def first_kernel(block, users, items, accum, ratings, ids_u, ids_i, counts,
                 user_out, resid, copy_out, item_out, acc_out, send_out,
                 dense, live, item_total, sems):
    row = lax.axis_index("au")
    copies = rating_copies(ratings.at[0, 0, 0], dense, ids_u, ids_i, row, 0, sems, block)
    for copy in copies:
        copy.start()
    mark_live(live, ids_u, ids_i, counts, row, 0, items.shape[0] // block)
    for copy in copies:
        copy.wait()
    item, acc = stratum_body(users, items[...], accum[...], dense, live, resid, item_total,
                             user_out, copy_out, block)
    item_out[...] = item
    acc_out[...] = acc
    send_out[0] = item.astype(BF16)
    send_out[1] = acc.astype(BF16)


def second_kernel(block, users, state, ratings, ids_u, ids_i, counts,
                  user_out, resid, copy_out, send_out,
                  dense, live, item_total, sems):
    row = lax.rem(lax.axis_index("au") + 1, lax.axis_size("au"))
    copies = rating_copies(ratings, dense, ids_u, ids_i, row, 1, sems, block)
    for copy in copies:
        copy.start()
    item_blocks = state.shape[1] // block
    mark_live(live, ids_u, ids_i, counts, row, 1, item_blocks)
    for copy in copies:
        copy.wait()
    item_first = state[0].astype(F32)
    acc_first = state[1].astype(F32)
    item, acc = stratum_body(users, item_first, acc_first, dense, live, resid, item_total,
                             user_out, copy_out, block)
    send_out[0] = (item - item_first).astype(BF16)
    send_out[1] = (acc - acc_first).astype(BF16)


def user_kernel(users, resid, item_copy, user_out):
    rows, width = users.shape
    inv_root = 1.0 / math.sqrt(width)
    for c in range(rows // CHUNK):
        span = pl.ds(c * CHUNK, CHUNK)
        total = dot_nn(resid[span, :], item_copy[...])
        user_out[span, :] = user_step(users[span, :], total, inv_root)


def vmem():
    return pl.BlockSpec(memory_space=pltpu.VMEM)


def smem():
    return pl.BlockSpec(memory_space=pltpu.SMEM)


def scratch(rows, cols, slots, live_count):
    return [
        pltpu.VMEM((rows, cols), BF16),
        pltpu.SMEM((live_count,), jnp.int32),
        pltpu.VMEM((cols, cols), F32),
        pltpu.SemaphoreType.DMA((slots,)),
    ]


def local(users, items, accum, ratings, block_users, block_items, block_counts):
    rows, width = users.shape
    cols = items.shape[0]
    slots, block = ratings.shape[3], ratings.shape[-1]
    live_count = (rows // block) * (cols // block)
    counts = jnp.transpose(block_counts, (1, 2, 0))
    n_au, n_ia = lax.axis_size("au"), lax.axis_size("ia")

    def at(a, i):
        return (a % n_au) * n_ia + i % n_ia

    places = [(a, i) for a in range(n_au) for i in range(n_ia)]
    out_pairs = [(at(a, i), at(a - 1, i + 1)) for a, i in places]
    back_pairs = [(target, source) for source, target in out_pairs]
    later = lax.ppermute(
        ratings[0, 0, 1], "au", [(a, (a - 1) % n_au) for a in range(n_au)]
    )
    shape = jax.ShapeDtypeStruct
    params = pltpu.CompilerParams(vmem_limit_bytes=24 << 20)
    user_mid, resid, item_copy, item_mid, acc_mid, sent = pl.pallas_call(
        functools.partial(first_kernel, block),
        out_shape=(
            shape((rows, width), F32),
            shape((rows, cols), BF16),
            shape((cols, width), BF16),
            shape((cols, width), F32),
            shape((cols, width), F32),
            shape((2, cols, width), BF16),
        ),
        in_specs=[vmem()] * 3 + [pl.BlockSpec(memory_space=pl.ANY)] + [smem()] * 3,
        out_specs=(vmem(),) * 6,
        scratch_shapes=scratch(rows, cols, slots, live_count),
        compiler_params=params,
    )(users, items, accum, ratings, block_users, block_items, counts)
    state = lax.ppermute(sent, ("au", "ia"), out_pairs)

    def finish(user_slab, residual, copy):
        return pl.pallas_call(
            user_kernel,
            out_shape=shape((rows, width), F32),
            in_specs=[vmem()] * 3,
            out_specs=vmem(),
            compiler_params=params,
        )(user_slab, residual, copy)

    user_mid = finish(user_mid, resid, item_copy)
    user_last, resid, item_copy, change = pl.pallas_call(
        functools.partial(second_kernel, block),
        out_shape=(
            shape((rows, width), F32),
            shape((rows, cols), BF16),
            shape((cols, width), BF16),
            shape((2, cols, width), BF16),
        ),
        in_specs=[vmem()] * 2 + [pl.BlockSpec(memory_space=pl.ANY)] + [smem()] * 3,
        out_specs=(vmem(),) * 4,
        scratch_shapes=scratch(rows, cols, slots, live_count),
        compiler_params=params,
    )(user_mid, state, later, block_users, block_items, counts)
    home = lax.ppermute(change, ("au", "ia"), back_pairs)
    user_last = finish(user_last, resid, item_copy)
    new_items = item_mid + home[0].astype(F32)
    new_accum = acc_mid + home[1].astype(F32)
    return user_last, new_items, new_accum


def solution(mesh):
    return jax.shard_map(
        local,
        mesh=mesh,
        in_specs=(
            P(("au", "ia"), None),
            P(("au", "ia"), None),
            P(("au", "ia"), None),
            P("au", "ia", None, None, None, None),
            P(None, "ia", None, None),
            P(None, "ia", None, None),
            P(None, "ia", None),
        ),
        out_specs=(P(("au", "ia"), None), P(("au", "ia"), None), P(("au", "ia"), None)),
        check_vma=False,
    )
```

time: 137 us -> 45.4 us (0.33)
  waiting for transfers between devices: 46 us -> 16.1 us
  matrix products: 29.6 us -> 0 us
  local copies, waits for them, and re-layouts: 27 us -> 7.91 us
  starting transfers between devices: 22.5 us -> 6.67 us
  Pallas kernels: 0 us -> 12.8 us
  other arithmetic: 9.28 us -> 0.84 us
    ppermute x6 -> x3, waiting for transfers between devices: 46 us -> 16.1 us  [the longest x1 8.88 us: local(): state = lax.ppermute(sent, ('au', 'ia'), out_pairs)]
    dot_general x28 -> x0, matrix products: 29.6 us -> none  [the longest x8 10.5 us: select_sum(): jnp.einsum(form, pick_table, low_half, preferred_element_type=jnp.float32)]
    ppermute x6 -> x3, starting transfers between devices: 22.5 us -> 6.67 us  [the longest x1 3.73 us: local(): lax.ppermute(ratings[0, 0, 1], 'au', [(a, (a - 1) % n_au) for a in range(...]
    pallas_call x0 -> x4, Pallas kernels: none -> 12.8 us  [the longest x1 5.17 us: local(): pl.pallas_call(functools.partial(second_kernel, block), out_shape=(shape(...]
    gather x8 -> x0, local copies, waits for them, and re-layouts: 10.6 us -> none  [the longest x4 6.01 us: block_sums(): user_rows = user_copy[user_ids]]
    convert_element_type x6 -> x0, other arithmetic: 5.4 us -> none  [the longest x4 3.55 us: stratum_update(): item_copy = item_slab.astype(jnp.bfloat16)]
    slice x3 -> x0, local copies, waits for them, and re-layouts: 3.5 us -> none  [the longest x1 1.4 us: local(): user_lists[:, stratum]]
    convert_element_type x3 -> x0, local copies, waits for them, and re-layouts: 3.02 us -> none  [stratum_update(): user_copy = user_slab.astype(jnp.bfloat16)]
  transfers between devices with their start and end apart: 6 -> 3, of which waited for: 4 -> 2; matrix products, arithmetic and copies ran while one was open for 13% -> 0% of each run, Pallas kernels for 0% -> 17%
where the time goes in v1:
time: 45.4 us; the launch traced here: 45 us
  waiting for transfers between devices  16.1 us (35%)
  Pallas kernels  12.8 us (28%)
  local copies, waits for them, and re-layouts  7.91 us (17%)
  starting transfers between devices  6.67 us (15%)
  other arithmetic  0.84 us (2%)
  between operations  0.68 us (1%)
    ppermute x1, waiting for transfers between devices, local(): state = lax.ppermute(sent, ('au', 'ia'), out_pairs)  8.88 us
    ppermute x1, waiting for transfers between devices, local(): home = lax.ppermute(change, ('au', 'ia'), back_pairs)  7.19 us
    unnamed x14, local copies, waits for them, and re-layouts  6.83 us
    pallas_call x1, Pallas kernels, local(): pl.pallas_call(functools.partial(second_kernel, block), out_shape=(shape(...  5.17 us
    pallas_call x1, Pallas kernels, local(): pl.pallas_call(functools.partial(first_kernel, block), out_shape=(shape((...  5.12 us
    ppermute x1, starting transfers between devices, local(): lax.ppermute(ratings[0, 0, 1], 'au', [(a, (a - 1) % n_au) for a in range(...  3.73 us
    ppermute x1, starting transfers between devices, local(): state = lax.ppermute(sent, ('au', 'ia'), out_pairs)  2.87 us
    pallas_call x2, Pallas kernels, finish(): pl.pallas_call(user_kernel, out_shape=shape((rows, width), F32), in_specs...  2.5 us
  transfers between devices with their start and end apart: 3, of which 2 were waited for; matrix products, arithmetic and copies ran while one was open for 0% of the time, Pallas kernels for 17%

profile of v1, /device:TPU:0, one launch (start us, length us, event | category | flops | bytes accessed | tf_op | source)
XLA Modules:
  0.0 45.0 jit_solution(12639654036042880480)
XLA Ops:
  0.6 1.1 %slice_bitcast_fusion = bf16[16,128,128]{2,1,0:T(8,128)(2,1)S(1)} fusion(bf16[1,1,2,16,128,128]{5,4,3,2,1,0:T(8,128)(2,1)} %ratings.1), kind=kLoop, calls=%fused_computation | loop fusion | bytes 1048576 | tf_op jit(solution)/shard_map/squeeze | solution.py:181
  1.7 3.7 %collective-permute-start.1 = (bf16[16,128,128]{2,1,0:T(8,128)(2,1)S(1)}, bf16[16,128,128]{2,1,0:T(8,128)(2,1)S(1)}, u32[]{:S(2)}, u32[]{:S(2)}) collective-permute-start(bf16[16,128,128]{2,1,0:T(8,128)(2,1)S(1)} %slice_bitcast_fusion), channel_id=1, source_target_pairs={{0,120},{8,0},{16,8},{24,16},{32,24},{40,32},{48,40},{56,48},{64,5... | collective-permute-start | bytes 1572872 | tf_op jit(solution)/shard_map/ppermute | solution.py:180
  5.5 0.0 copy-start
  5.5 1.2 %copy-done = bf16[1,1,2,16,128,128]{5,4,3,2,1,0:T(8,128)(2,1)S(1)} copy-done((bf16[1,1,2,16,128,128]{5,4,3,2,1,0:T(8,128)(2,1)S(1)}, bf16[1,1,2,16,128,128]{5,4,3,2,1,0:T(8,128)(2,1)}, u32[]{:S(2)}) %copy-start) | copy-done | bytes 1048600
  6.7 0.0 copy-start.1
  6.7 1.6 %copy-done.1 = f32[2048,256]{1,0:T(8,128)S(1)} copy-done((f32[2048,256]{1,0:T(8,128)S(1)}, f32[2048,256]{1,0:T(8,128)}, u32[]{:S(2)}) %copy-start.1) | copy-done | bytes 2097176
  8.3 0.0 copy-start.2
  8.3 0.9 %copy-done.2 = f32[256,256]{1,0:T(8,128)S(1)} copy-done((f32[256,256]{1,0:T(8,128)S(1)}, f32[256,256]{1,0:T(8,128)}, u32[]{:S(2)}) %copy-start.2) | copy-done | bytes 262168
  9.2 0.0 copy-start.3
  9.2 0.9 %copy-done.3 = f32[256,256]{1,0:T(8,128)S(1)} copy-done((f32[256,256]{1,0:T(8,128)S(1)}, f32[256,256]{1,0:T(8,128)}, u32[]{:S(2)}) %copy-start.3) | copy-done | bytes 262168
  10.2 0.0 copy-start.4
  10.2 0.7 %copy-done.4 = s32[16,1,2,16]{3,2,1,0:T(2,128)S(1)} copy-done((s32[16,1,2,16]{3,2,1,0:T(2,128)S(1)}, s32[16,1,2,16]{3,2,1,0:T(2,128)}, u32[]{:S(2)}) %copy-start.4) | copy-done | bytes 2072
  10.9 0.0 copy-start.5
  10.9 0.7 %copy-done.5 = s32[16,1,2,16]{3,2,1,0:T(2,128)S(1)} copy-done((s32[16,1,2,16]{3,2,1,0:T(2,128)S(1)}, s32[16,1,2,16]{3,2,1,0:T(2,128)}, u32[]{:S(2)}) %copy-start.5) | copy-done | bytes 2072
  11.6 0.0 copy-start.6
  11.6 0.7 %copy-done.6 = s32[16,1,2]{0,2,1:T(2,128)S(1)} copy-done((s32[16,1,2]{0,2,1:T(2,128)S(1)}, s32[16,1,2]{0,2,1:T(2,128)}, u32[]{:S(2)}) %copy-start.6) | copy-done | bytes 152
  12.3 5.1 %shard_map.94 = (f32[2048,256]{1,0:T(8,128)S(1)}, bf16[2048,256]{1,0:T(8,128)(2,1)S(1)}, bf16[256,256]{1,0:T(8,128)(2,1)S(1)}, f32[256,256]{1,0:T(8,128)S(1)}, f...) custom-call(f32[2048,256]{1,0:T(8,128)S(1)} %copy-done.1, f32[256,256]{1,0:T(8,128)S(1)} %copy-done.2, ...), custom_call_target="tpu_custom_call" | custom-call | tf_op jit(solution)/shard_map/pallas_call | solution.py:185
  17.4 2.9 %collective-permute-start = (bf16[2,256,256]{2,1,0:T(8,128)(2,1)S(1)}, bf16[2,256,256]{2,1,0:T(8,128)(2,1)S(1)}, u32[]{:S(2)}, u32[]{:S(2)}) collective-permute-start(bf16[2,256,256]{2,1,0:T(8,128)(2,1)S(1)} %get-tuple-element.16), channel_id=1, source_target_pairs={{0,121},{1,122},{2,123},{3,124},{4,125},{5,126},{6,127},{7,120},{8... | collective-permute-start | bytes 786440 | tf_op jit(solution)/shard_map/ppermute | solution.py:200
  20.3 0.6 %shard_map.95.users = f32[2048,256]{1,0:T(8,128)S(1)} custom-call(f32[2048,256]{1,0:T(8,128)S(1)} %get-tuple-element.13.users, bf16[2048,256]{1,0:T(8,128)(2,1)S(1)} %get-tuple-element.14.resid, bf16[256,256]{1,0:T(8,128)(2,1)S(1)} %get-tuple-element.15.item_copy), custom_call_target="tpu_custom_call" | custom-call | tf_op jit(solution)/shard_map/pallas_call | solution.py:203
  20.9 8.9 %collective-permute-done.state = bf16[2,256,256]{2,1,0:T(8,128)(2,1)S(1)} collective-permute-done((bf16[2,256,256]{2,1,0:T(8,128)(2,1)S(1)}, bf16[2,256,256]{2,1,0:T(8,128)(2,1)S(1)}, u32[]{:S(2)}, u32[]{:S(2)}) %collective-permute-start) | collective-permute-done | bytes 262176 | tf_op jit(solution)/shard_map/ppermute | solution.py:200
  29.8 0.0 collective-permute-done.1.ratings
  29.8 5.2 %shard_map.96 = (f32[2048,256]{1,0:T(8,128)S(1)}, bf16[2048,256]{1,0:T(8,128)(2,1)S(1)}, bf16[256,256]{1,0:T(8,128)(2,1)S(1)}, bf16[2,256,256]{2,1,0:T(8,128)(2,1)S(1)}) custom-call(f32[2048,256]{1,0:T(8,128)S(1)} %shard_map.95.users, bf16[2,256,256]{2,1,0:T(8,128)(2,1)S(1)} %collective-permute-done.state, ...), custom_call_target="tpu_custom_call" | custom-call | tf_op jit(solution)/shard_map/pallas_call | solution.py:212
  34.9 0.1 collective-permute-start.2
  35.0 1.9 %shard_map.97 = f32[2048,256]{1,0:T(8,128)} custom-call(f32[2048,256]{1,0:T(8,128)S(1)} %get-tuple-element.17.users, bf16[2048,256]{1,0:T(8,128)(2,1)S(1)} %get-tuple-element.18.resid, bf16[256,256]{1,0:T(8,128)(2,1)S(1)} %get-tuple-element.19.item_copy), custom_call_target="tpu_custom_call" | custom-call | tf_op jit(solution)/shard_map/pallas_call | solution.py:203
  36.9 7.2 %collective-permute-done.2 = bf16[2,256,256]{2,1,0:T(8,128)(2,1)S(1)} collective-permute-done((bf16[2,256,256]{2,1,0:T(8,128)(2,1)S(1)}, bf16[2,256,256]{2,1,0:T(8,128)(2,1)S(1)}, u32[]{:S(2)}, u32[]{:S(2)}) %collective-permute-start.2) | collective-permute-done | bytes 262176 | tf_op jit(solution)/shard_map/ppermute | solution.py:225
  44.1 0.8 %convert_add_fusion = (f32[256,256]{1,0:T(8,128)}, f32[256,256]{1,0:T(8,128)}) fusion(f32[256,256]{1,0:T(8,128)S(1)} %get-tuple-element.22, bf16[2,256,256]{2,1,0:T(8,128)(2,1)S(1)} %collective-permute-done.2, f32[256,256]{1,0:T(8,128)S(1)} %get-tuple-element.20), kind=kLoop, calls=%fused_computation.1 | loop fusion | flops 262144 | bytes 1310720 | tf_op jit(solution)/shard_map/add | solution.py:228
Async XLA Ops:
  1.7 28.0 %collective-permute-start.1 = (bf16[16,128,128]{2,1,0:T(8,128)(2,1)S(1)}, bf16[16,128,128]{2,1,0:T(8,128)(2,1)S(1)}, u32[]{:S(2)}, u32[]{:S(2)}) collective-permute-start(bf16[16,128,128]{2,1,0:T(8,128)(2,1)S(1)} %slice_bitcast_fusion), channel_id=1, source_target_pairs={{0,120},{8,0},{16,8},{24,16},{32,24},{40,32},{48,40},{56,48},{64,5... | collective-permute-start | bytes 1572872 | tf_op jit(solution)/shard_map/ppermute | solution.py:180
  5.5 1.2 %copy-start = (bf16[1,1,2,16,128,128]{5,4,3,2,1,0:T(8,128)(2,1)S(1)}, bf16[1,1,2,16,128,128]{5,4,3,2,1,0:T(8,128)(2,1)}, u32[]{:S(2)}) copy-start(bf16[1,1,2,16,128,128]{5,4,3,2,1,0:T(8,128)(2,1)} %ratings.1) | copy-start | bytes 3145732
  6.7 1.6 %copy-start.1 = (f32[2048,256]{1,0:T(8,128)S(1)}, f32[2048,256]{1,0:T(8,128)}, u32[]{:S(2)}) copy-start(f32[2048,256]{1,0:T(8,128)} %users.1) | copy-start | bytes 6291460
  8.3 0.9 %copy-start.2 = (f32[256,256]{1,0:T(8,128)S(1)}, f32[256,256]{1,0:T(8,128)}, u32[]{:S(2)}) copy-start(f32[256,256]{1,0:T(8,128)} %items.1) | copy-start | bytes 786436
  9.2 0.9 %copy-start.3 = (f32[256,256]{1,0:T(8,128)S(1)}, f32[256,256]{1,0:T(8,128)}, u32[]{:S(2)}) copy-start(f32[256,256]{1,0:T(8,128)} %accum.1) | copy-start | bytes 786436
  10.2 0.7 %copy-start.4 = (s32[16,1,2,16]{3,2,1,0:T(2,128)S(1)}, s32[16,1,2,16]{3,2,1,0:T(2,128)}, u32[]{:S(2)}) copy-start(s32[16,1,2,16]{3,2,1,0:T(2,128)} %ids_u.3) | copy-start | bytes 6148
  10.9 0.7 %copy-start.5 = (s32[16,1,2,16]{3,2,1,0:T(2,128)S(1)}, s32[16,1,2,16]{3,2,1,0:T(2,128)}, u32[]{:S(2)}) copy-start(s32[16,1,2,16]{3,2,1,0:T(2,128)} %ids_i.3) | copy-start | bytes 6148
  11.6 0.7 %copy-start.6 = (s32[16,1,2]{0,2,1:T(2,128)S(1)}, s32[16,1,2]{0,2,1:T(2,128)}, u32[]{:S(2)}) copy-start(s32[16,1,2]{0,2,1:T(2,128)} %param.13) | copy-start | bytes 388
  17.4 12.3 %collective-permute-start = (bf16[2,256,256]{2,1,0:T(8,128)(2,1)S(1)}, bf16[2,256,256]{2,1,0:T(8,128)(2,1)S(1)}, u32[]{:S(2)}, u32[]{:S(2)}) collective-permute-start(bf16[2,256,256]{2,1,0:T(8,128)(2,1)S(1)} %get-tuple-element.16), channel_id=1, source_target_pairs={{0,121},{1,122},{2,123},{3,124},{4,125},{5,126},{6,127},{7,120},{8... | collective-permute-start | bytes 786440 | tf_op jit(solution)/shard_map/ppermute | solution.py:200
  34.9 9.2 %collective-permute-start.2 = (bf16[2,256,256]{2,1,0:T(8,128)(2,1)S(1)}, bf16[2,256,256]{2,1,0:T(8,128)(2,1)S(1)}, u32[]{:S(2)}, u32[]{:S(2)}) collective-permute-start(bf16[2,256,256]{2,1,0:T(8,128)(2,1)S(1)} %get-tuple-element.21), channel_id=1, source_target_pairs={{121,0},{122,1},{123,2},{124,3},{125,4},{126,5},{127,6},{120,7},{1... | collective-permute-start | bytes 786440 | tf_op jit(solution)/shard_map/ppermute | solution.py:225

commit v2 on v0

v2 whole, which is shorter than its diff:
```python
import functools
import math

import jax
import jax.numpy as jnp
from jax import lax
from jax.experimental import pallas as pl
from jax.experimental.pallas import tpu as pltpu
from jax.sharding import PartitionSpec as P

rate_users = 0.1
rate_items = 0.1
weight_decay = 0.02
adagrad_eps = 1e-08

CHUNK = 1024
F32 = jnp.float32
BF16 = jnp.bfloat16
TILE = 16


def dot(left, right, dims):
    return lax.dot_general(left, right, (dims, ((), ())), preferred_element_type=F32)


def rating_copies(source, dense, ids_u, ids_i, stratum, sems, block):
    copies = []
    for n in range(source.shape[0]):
        user_at = pl.multiple_of(ids_u[0, 0, stratum, n] * block, block)
        item_at = pl.multiple_of(ids_i[0, 0, stratum, n] * block, block)
        copies.append(
            pltpu.make_async_copy(
                source.at[n], dense.at[pl.ds(user_at, block), pl.ds(item_at, block)], sems.at[n]
            )
        )
    return copies


def fill_mask(mask, ids_u, ids_i, counts, stratum, row, item_blocks):
    mask[...] = jnp.zeros(mask.shape, BF16)
    for n in range(ids_u.shape[-1]):
        code = ids_u[0, 0, stratum, n] * item_blocks + ids_i[0, 0, stratum, n]
        live = jnp.where(n < counts[0, stratum, row], 1.0, 0.0)
        mask[code] = jnp.full(mask.shape[1:], live, F32).astype(BF16)


def id_copies(ids_u, ids_i, counts, ids_u_s, ids_i_s, counts_s, row, sems):
    here = pl.ds(row, 1)
    return [
        pltpu.make_async_copy(ids_u.at[here], ids_u_s, sems.at[0]),
        pltpu.make_async_copy(ids_i.at[here], ids_i_s, sems.at[1]),
        pltpu.make_async_copy(counts, counts_s, sems.at[2]),
    ]


def load_kernel(block, users, items, accum, ratings, ids_u, ids_i, counts,
                users_out, items_out, accum_out, later_out, dense, mask,
                ids_u_s, ids_i_s, counts_s, id_sems, data_sems, sems):
    row = lax.axis_index("au")
    small = id_copies(ids_u, ids_i, counts, ids_u_s, ids_i_s, counts_s, row, id_sems)
    large = [
        pltpu.make_async_copy(ratings.at[0, 0, 1], later_out, data_sems.at[0]),
        pltpu.make_async_copy(items, items_out, data_sems.at[1]),
        pltpu.make_async_copy(accum, accum_out, data_sems.at[2]),
        pltpu.make_async_copy(users, users_out, data_sems.at[3]),
    ]
    for copy in small + large:
        copy.start()
    for copy in small:
        copy.wait()
    slots = rating_copies(ratings.at[0, 0, 0], dense, ids_u_s, ids_i_s, 0, sems, block)
    for copy in slots:
        copy.start()
    fill_mask(mask, ids_u_s, ids_i_s, counts_s, 0, row, items.shape[0] // block)
    for copy in large + slots:
        copy.wait()


def residual_chunk(predicted, dense, mask, first, block, out):
    rows, cols = predicted.shape
    value = (dense[pl.ds(first, rows), :].astype(F32) - predicted).astype(BF16)
    for r in range(rows // block):
        for c in range(cols // block):
            part = value[r * block : (r + 1) * block, c * block : (c + 1) * block]
            flag = mask[(first // block + r) * (cols // block) + c]
            flag = jnp.concatenate([flag] * (block // TILE), axis=0)
            out[pl.ds(first + r * block, block), pl.ds(c * block, block)] = jnp.where(
                flag != 0, part, jnp.zeros_like(part)
            )


def sgd_step(source, scaled, dense, mask, resid, copies, user_out, block):
    rows = source.shape[0]
    for c in range(rows // CHUNK):
        span = pl.ds(c * CHUNK, CHUNK)
        user = source[span, :]
        user_copy = user.astype(BF16)
        copies[span, :] = user_copy
        predicted = dot(user_copy, scaled, ((1,), (1,)))
        residual_chunk(predicted, dense, mask, c * CHUNK, block, resid)
        if user_out is not None:
            user_out[span, :] = user_step(user, dot(resid[span, :], scaled, ((1,), (0,))))
    return dot(resid[...], copies[...], ((0,), (0,)))


def user_step(user, scaled_total):
    return (1.0 - rate_users * weight_decay) * user + rate_users * scaled_total


def item_step(item, acc, total):
    grad = weight_decay * item - (1.0 / math.sqrt(item.shape[-1])) * total
    acc = acc + grad * grad
    return item - rate_items * grad / jnp.sqrt(acc + adagrad_eps), acc


def scale(item):
    return item.astype(BF16) * BF16(1.0 / math.sqrt(item.shape[-1]))


def user_update(users, resid, scaled, user_out):
    for c in range(users.shape[0] // CHUNK):
        span = pl.ds(c * CHUNK, CHUNK)
        user_out[span, :] = user_step(users[span, :], dot(resid[span, :], scaled[...], ((1,), (0,))))


def first_kernel(block, users, items, accum, dense, mask,
                 user_out, resid, scaled_out, item_out, acc_out, item_send, acc_send, copies):
    item = items[...]
    total = sgd_step(users, scale(item), dense, mask, resid, copies, user_out, block)
    item, acc = item_step(item, accum[...], total)
    scaled = scale(item)
    scaled_out[...] = scaled
    total = sgd_step(user_out, scaled, dense, mask, resid, copies, None, block)
    item, acc = item_step(item, acc, total)
    item_out[...] = item
    acc_out[...] = acc
    item_send[...] = item.astype(BF16)
    acc_send[...] = acc.astype(BF16)


def turn_kernel(block, users, resid, scaled, later, ids_u, ids_i, counts, user_out, dense, mask,
                ids_u_s, ids_i_s, counts_s, id_sems, sems):
    row = lax.rem(lax.axis_index("au") + 1, lax.axis_size("au"))
    small = id_copies(ids_u, ids_i, counts, ids_u_s, ids_i_s, counts_s, row, id_sems)
    for copy in small:
        copy.start()
    for copy in small:
        copy.wait()
    slots = rating_copies(later, dense, ids_u_s, ids_i_s, 1, sems, block)
    for copy in slots:
        copy.start()
    fill_mask(mask, ids_u_s, ids_i_s, counts_s, 1, row, dense.shape[1] // block)
    user_update(users, resid, scaled, user_out)
    for copy in slots:
        copy.wait()


def second_kernel(block, users, items, dense, mask, user_out, total_out, resid, copies):
    scaled = scale(items[...].astype(F32))
    total_out[...] = sgd_step(users, scaled, dense, mask, resid, copies, user_out, block)


def third_kernel(block, users, items, accum, total, dense, mask,
                 resid, scaled_out, send, copies):
    item_first = items[...].astype(F32)
    acc_first = accum[...].astype(F32)
    item, acc = item_step(item_first, acc_first, total[...])
    scaled = scale(item)
    scaled_out[...] = scaled
    again = sgd_step(users, scaled, dense, mask, resid, copies, None, block)
    item, acc = item_step(item, acc, again)
    send[0] = (item - item_first).astype(BF16)
    send[1] = (acc - acc_first).astype(BF16)


def vmem(count):
    return [pl.BlockSpec(memory_space=pltpu.VMEM)] * count


def hbm(count):
    return [pl.BlockSpec(memory_space=pltpu.HBM)] * count


def call(body, in_specs, outs, scratch, args):
    return pl.pallas_call(
        body,
        out_shape=tuple(jax.ShapeDtypeStruct(shape, dtype) for shape, dtype in outs),
        in_specs=in_specs,
        out_specs=tuple(vmem(len(outs))),
        scratch_shapes=scratch,
        compiler_params=pltpu.CompilerParams(vmem_limit_bytes=24 << 20),
    )(*args)


def in_hbm(*values):
    return [pltpu.with_memory_space_constraint(value, pltpu.HBM) for value in values]


def local(users, items, accum, ratings, block_users, block_items, block_counts):
    rows, width = users.shape
    cols = items.shape[0]
    strata, slots, block = ratings.shape[2], ratings.shape[3], ratings.shape[-1]
    counts = jnp.transpose(block_counts, (1, 2, 0))
    n_au, n_ia = lax.axis_size("au"), lax.axis_size("ia")
    user_shape, item_shape = ((rows, width), F32), ((cols, width), F32)
    resid_shape, copy_shape = ((rows, cols), BF16), ((cols, width), BF16)
    slots_shape = ((slots, block, block), BF16)
    mask_shape = (((rows // block) * (cols // block), TILE, block), BF16)
    user_copies = pltpu.VMEM((rows, width), BF16)
    dma = pltpu.SemaphoreType.DMA
    ids_smem = pltpu.SMEM((1, 1, strata, slots), jnp.int32)

    def at(a, i):
        return (a % n_au) * n_ia + i % n_ia

    places = [(a, i) for a in range(n_au) for i in range(n_ia)]
    out_pairs = [(at(a, i), at(a - 1, i + 1)) for a, i in places]
    back_pairs = [(target, source) for source, target in out_pairs]

    tables = [ids_smem, ids_smem, pltpu.SMEM(counts.shape, jnp.int32), dma((3,))]
    user, item, acc, later, dense, mask = call(
        functools.partial(load_kernel, block),
        hbm(7),
        (user_shape, item_shape, item_shape, slots_shape, resid_shape, mask_shape),
        tables + [dma((4,)), dma((slots,))],
        in_hbm(users, items, accum, ratings, block_users, block_items, counts),
    )
    later = lax.ppermute(later, "au", [(a, (a - 1) % n_au) for a in range(n_au)])
    user, resid, scaled, item_mid, acc_mid, item_sent, acc_sent = call(
        functools.partial(first_kernel, block),
        vmem(5),
        (user_shape, resid_shape, copy_shape, item_shape, item_shape, copy_shape, copy_shape),
        [user_copies],
        (user, item, acc, dense, mask),
    )
    item_here = lax.ppermute(item_sent, ("au", "ia"), out_pairs)
    acc_here = lax.ppermute(acc_sent, ("au", "ia"), out_pairs)
    user, dense, mask = call(
        functools.partial(turn_kernel, block),
        vmem(4) + hbm(3),
        (user_shape, resid_shape, mask_shape),
        tables + [dma((slots,))],
        [user, resid, scaled, later] + in_hbm(block_users, block_items, counts),
    )
    user, total = call(
        functools.partial(second_kernel, block),
        vmem(4),
        (user_shape, item_shape),
        [pltpu.VMEM(*resid_shape), user_copies],
        (user, item_here, dense, mask),
    )
    resid, scaled, change = call(
        functools.partial(third_kernel, block),
        vmem(6),
        (resid_shape, copy_shape, ((2, cols, width), BF16)),
        [user_copies],
        (user, item_here, acc_here, total, dense, mask),
    )
    home = lax.ppermute(change, ("au", "ia"), back_pairs)
    (user,) = call(user_update, vmem(3), (user_shape,), [], (user, resid, scaled))
    return user, item_mid + home[0].astype(F32), acc_mid + home[1].astype(F32)


def solution(mesh):
    return jax.shard_map(
        local,
        mesh=mesh,
        in_specs=(
            P(("au", "ia"), None),
            P(("au", "ia"), None),
            P(("au", "ia"), None),
            P("au", "ia", None, None, None, None),
            P(None, "ia", None, None),
            P(None, "ia", None, None),
            P(None, "ia", None),
        ),
        out_specs=(P(("au", "ia"), None), P(("au", "ia"), None), P(("au", "ia"), None)),
        check_vma=False,
    )
```

time: 137 us -> 34.4 us (0.25); the launches traced: 135 us -> 34.2 us
  waiting for transfers between devices: 46 us -> 13.7 us
  matrix products: 29.6 us -> 0 us
  local copies, waits for them, and re-layouts: 27 us -> 0 us
  starting transfers between devices: 22.5 us -> 8.49 us
  Pallas kernels: 0 us -> 10.6 us
  other arithmetic: 9.28 us -> 0.84 us
    ppermute x6 -> x4, waiting for transfers between devices: 46 us -> 13.7 us  [the longest x1 6.69 us: local(): home = lax.ppermute(change, ('au', 'ia'), back_pairs)]
    dot_general x28 -> x0, matrix products: 29.6 us -> none  [the longest x8 10.5 us: select_sum(): jnp.einsum(form, pick_table, low_half, preferred_element_type=jnp.float32)]
    ppermute x6 -> x4, starting transfers between devices: 22.5 us -> 8.49 us  [the longest x1 3.73 us: local(): lax.ppermute(later, 'au', [(a, (a - 1) % n_au) for a in range(n_au)])]
    pallas_call x0 -> x6, Pallas kernels: none -> 10.6 us  [call(): pl.pallas_call(body, out_shape=tuple((jax.ShapeDtypeStruct(shape, dtype)...]
    gather x8 -> x0, local copies, waits for them, and re-layouts: 10.6 us -> none  [the longest x4 6.01 us: block_sums(): user_rows = user_copy[user_ids]]
    unnamed x58 -> x0, local copies, waits for them, and re-layouts: 5.62 us -> none
    convert_element_type x6 -> x0, other arithmetic: 5.4 us -> none  [the longest x4 3.55 us: stratum_update(): item_copy = item_slab.astype(jnp.bfloat16)]
    slice x3 -> x0, local copies, waits for them, and re-layouts: 3.5 us -> none  [the longest x1 1.4 us: local(): user_lists[:, stratum]]
  transfers between devices with their start and end apart: 6 -> 4, of which waited for: 4 -> 4; matrix products, arithmetic and copies ran while one was open for 13% -> 0% of each run, Pallas kernels for 0% -> 20%
where the time goes in v2:
time: 34.4 us; the launch traced here: 34.2 us
  waiting for transfers between devices  13.7 us (40%)
  Pallas kernels  10.6 us (31%)
  starting transfers between devices  8.49 us (25%)
  other arithmetic  0.84 us (2%)
  between operations  0.67 us (2%)
    pallas_call x6, Pallas kernels, call(): pl.pallas_call(body, out_shape=tuple((jax.ShapeDtypeStruct(shape, dtype)...  10.6 us
    ppermute x1, waiting for transfers between devices, local(): home = lax.ppermute(change, ('au', 'ia'), back_pairs)  6.69 us
    ppermute x1, waiting for transfers between devices, local(): acc_here = lax.ppermute(acc_sent, ('au', 'ia'), out_pairs)  4.14 us
    ppermute x1, starting transfers between devices, local(): lax.ppermute(later, 'au', [(a, (a - 1) % n_au) for a in range(n_au)])  3.73 us
    ppermute x1, starting transfers between devices, local(): item_here = lax.ppermute(item_sent, ('au', 'ia'), out_pairs)  2.87 us
    ppermute x1, waiting for transfers between devices, local(): item_here = lax.ppermute(item_sent, ('au', 'ia'), out_pairs)  2.64 us
    ppermute x1, starting transfers between devices, local(): acc_here = lax.ppermute(acc_sent, ('au', 'ia'), out_pairs)  1.19 us
    add x1, other arithmetic, local(): return (user, item_mid + home[0].astype(F32), acc_mid + home[1].astype(F32))  0.84 us
  transfers between devices with their start and end apart: 4, of which 4 were waited for; matrix products, arithmetic and copies ran while one was open for 0% of the time, Pallas kernels for 20%

profile of v2, /device:TPU:0, one launch (start us, length us, event | category | flops | bytes accessed | tf_op | source)
XLA Modules:
  0.0 34.2 jit_solution(4050487952491734111)
XLA Ops:
  0.6 2.3 %shard_map.94 = (f32[2048,256]{1,0:T(8,128)S(1)}, f32[256,256]{1,0:T(8,128)S(1)}, f32[256,256]{1,0:T(8,128)S(1)}, bf16[16,128,128]{2,1,0:T(8,128)(2,1)S(1)}, bf1...) custom-call(f32[2048,256]{1,0:T(8,128)} %users.1, f32[256,256]{1,0:T(8,128)} %items.1, f32[256,256]{1,0:T(8,128)} %accum.1, ...), custom_call_target="tpu_custom_call" | custom-call | tf_op jit(solution)/shard_map/pallas_call | solution.py:185
  2.9 3.7 %collective-permute-start = (bf16[16,128,128]{2,1,0:T(8,128)(2,1)S(1)}, bf16[16,128,128]{2,1,0:T(8,128)(2,1)S(1)}, u32[]{:S(2)}, u32[]{:S(2)}) collective-permute-start(bf16[16,128,128]{2,1,0:T(8,128)(2,1)S(1)} %get-tuple-element.32), channel_id=1, source_target_pairs={{0,120},{8,0},{16,8},{24,16},{32,24},{40,32},{48,40},{56,48},{64,5... | collective-permute-start | bytes 1572872 | tf_op jit(solution)/shard_map/ppermute | solution.py:228
  6.6 2.5 %shard_map.95 = (f32[2048,256]{1,0:T(8,128)S(1)}, bf16[2048,256]{1,0:T(8,128)(2,1)S(1)}, bf16[256,256]{1,0:T(8,128)(2,1)S(1)}, f32[256,256]{1,0:T(8,128)S(1)}, f...) custom-call(f32[2048,256]{1,0:T(8,128)S(1)} %get-tuple-element.24.users, ...), custom_call_target="tpu_custom_call" | custom-call | tf_op jit(solution)/shard_map/pallas_call | solution.py:185
  9.1 2.9 %collective-permute-start.1 = (bf16[256,256]{1,0:T(8,128)(2,1)S(1)}, bf16[256,256]{1,0:T(8,128)(2,1)S(1)}, u32[]{:S(2)}, u32[]{:S(2)}) collective-permute-start(bf16[256,256]{1,0:T(8,128)(2,1)S(1)} %get-tuple-element.34), channel_id=1, source_target_pairs={{0,121},{1,122},{2,123},{3,124},{4,125},{5,126},{6,127},{7,120},{8... | collective-permute-start | bytes 393224 | tf_op jit(solution)/shard_map/ppermute | solution.py:236
  12.0 1.2 %collective-permute-start.2 = (bf16[256,256]{1,0:T(8,128)(2,1)S(1)}, bf16[256,256]{1,0:T(8,128)(2,1)S(1)}, u32[]{:S(2)}, u32[]{:S(2)}) collective-permute-start(bf16[256,256]{1,0:T(8,128)(2,1)S(1)} %get-tuple-element.38), channel_id=1, source_target_pairs={{0,121},{1,122},{2,123},{3,124},{4,125},{5,126},{6,127},{7,120},{8... | collective-permute-start | bytes 393224 | tf_op jit(solution)/shard_map/ppermute | solution.py:237
  13.2 0.2 collective-permute-done.later
  13.3 1.6 %shard_map.96 = (f32[2048,256]{1,0:T(8,128)S(1)}, bf16[2048,256]{1,0:T(8,128)(2,1)S(1)}, bf16[32,16,128]{2,1,0:T(8,128)(2,1)S(1)}) custom-call(f32[2048,256]{1,0:T(8,128)S(1)} %get-tuple-element.29.users, bf16[2048,256]{1,0:T(8,128)(2,1)S(1)} %get-tuple-element.30.resid, bf16[256,256]{1,0:T(8,128)(2,1)S(1)} %get-tuple-element.31.scaled, ...), custom_call_target="tpu_custom_call" | custom-call | tf_op jit(solution)/shard_map/pallas_call | solution.py:185
  14.9 2.6 %collective-permute-done.1.items = bf16[256,256]{1,0:T(8,128)(2,1)S(1)} collective-permute-done((bf16[256,256]{1,0:T(8,128)(2,1)S(1)}, bf16[256,256]{1,0:T(8,128)(2,1)S(1)}, u32[]{:S(2)}, u32[]{:S(2)}) %collective-permute-start.1) | collective-permute-done | bytes 131104 | tf_op jit(solution)/shard_map/ppermute | solution.py:236
  17.5 1.1 %shard_map.97 = (f32[2048,256]{1,0:T(8,128)S(1)}, f32[256,256]{1,0:T(8,128)S(1)}) custom-call(f32[2048,256]{1,0:T(8,128)S(1)} %get-tuple-element.33.users, bf16[256,256]{1,0:T(8,128)(2,1)S(1)} %collective-permute-done.1.items, bf16[2048,256]{1,0:T(8,128)(2,1)S(1)} %get-tuple-element.35.dense, bf16[32,16,128]{2,1,0:T(8,128)(2,1)S(1)} %get-tuple-element.36.mask), custom_call_target="tpu_custom_call" | custom-call | tf_op jit(solution)/shard_map/pallas_call | solution.py:185
  18.6 4.1 %collective-permute-done.2.accum = bf16[256,256]{1,0:T(8,128)(2,1)S(1)} collective-permute-done((bf16[256,256]{1,0:T(8,128)(2,1)S(1)}, bf16[256,256]{1,0:T(8,128)(2,1)S(1)}, u32[]{:S(2)}, u32[]{:S(2)}) %collective-permute-start.2) | collective-permute-done | bytes 131104 | tf_op jit(solution)/shard_map/ppermute | solution.py:237
  22.8 1.4 %shard_map.98 = (bf16[2048,256]{1,0:T(8,128)(2,1)S(1)}, bf16[256,256]{1,0:T(8,128)(2,1)S(1)}, bf16[2,256,256]{2,1,0:T(8,128)(2,1)S(1)}) custom-call(f32[2048,256]{1,0:T(8,128)S(1)} %get-tuple-element.37.users, bf16[256,256]{1,0:T(8,128)(2,1)S(1)} %collective-permute-done.1.items, bf16[256,256]{1,0:T(8,128)(2,1)S(1)} %collective-permute-done.2.accum, ...), custom_call_target="tpu_custom_call" | custom-call | tf_op jit(solution)/shard_map/pallas_call | solution.py:185
  24.2 0.7 %collective-permute-start.3 = (bf16[2,256,256]{2,1,0:T(8,128)(2,1)S(1)}, bf16[2,256,256]{2,1,0:T(8,128)(2,1)S(1)}, u32[]{:S(2)}, u32[]{:S(2)}) collective-permute-start(bf16[2,256,256]{2,1,0:T(8,128)(2,1)S(1)} %get-tuple-element.43), channel_id=1, source_target_pairs={{121,0},{122,1},{123,2},{124,3},{125,4},{126,5},{127,6},{120,7},{1... | collective-permute-start | bytes 786440 | tf_op jit(solution)/shard_map/ppermute | solution.py:259
  24.9 1.8 %shard_map.99 = f32[2048,256]{1,0:T(8,128)} custom-call(f32[2048,256]{1,0:T(8,128)S(1)} %get-tuple-element.37.users, bf16[2048,256]{1,0:T(8,128)(2,1)S(1)} %get-tuple-element.40.resid, bf16[256,256]{1,0:T(8,128)(2,1)S(1)} %get-tuple-element.41.scaled), custom_call_target="tpu_custom_call" | custom-call | tf_op jit(solution)/shard_map/pallas_call | solution.py:185
  26.7 6.7 %collective-permute-done.3 = bf16[2,256,256]{2,1,0:T(8,128)(2,1)S(1)} collective-permute-done((bf16[2,256,256]{2,1,0:T(8,128)(2,1)S(1)}, bf16[2,256,256]{2,1,0:T(8,128)(2,1)S(1)}, u32[]{:S(2)}, u32[]{:S(2)}) %collective-permute-start.3) | collective-permute-done | bytes 262176 | tf_op jit(solution)/shard_map/ppermute | solution.py:259
  33.4 0.8 %convert_add_fusion = (f32[256,256]{1,0:T(8,128)}, f32[256,256]{1,0:T(8,128)}) fusion(f32[256,256]{1,0:T(8,128)S(1)} %get-tuple-element.44, bf16[2,256,256]{2,1,0:T(8,128)(2,1)S(1)} %collective-permute-done.3, f32[256,256]{1,0:T(8,128)S(1)} %get-tuple-element.42), kind=kLoop, calls=%fused_computation | loop fusion | flops 262144 | bytes 1310720 | tf_op jit(solution)/shard_map/add | solution.py:261
Async XLA Ops:
  2.9 10.4 %collective-permute-start = (bf16[16,128,128]{2,1,0:T(8,128)(2,1)S(1)}, bf16[16,128,128]{2,1,0:T(8,128)(2,1)S(1)}, u32[]{:S(2)}, u32[]{:S(2)}) collective-permute-start(bf16[16,128,128]{2,1,0:T(8,128)(2,1)S(1)} %get-tuple-element.32), channel_id=1, source_target_pairs={{0,120},{8,0},{16,8},{24,16},{32,24},{40,32},{48,40},{56,48},{64,5... | collective-permute-start | bytes 1572872 | tf_op jit(solution)/shard_map/ppermute | solution.py:228
  9.1 8.4 %collective-permute-start.1 = (bf16[256,256]{1,0:T(8,128)(2,1)S(1)}, bf16[256,256]{1,0:T(8,128)(2,1)S(1)}, u32[]{:S(2)}, u32[]{:S(2)}) collective-permute-start(bf16[256,256]{1,0:T(8,128)(2,1)S(1)} %get-tuple-element.34), channel_id=1, source_target_pairs={{0,121},{1,122},{2,123},{3,124},{4,125},{5,126},{6,127},{7,120},{8... | collective-permute-start | bytes 393224 | tf_op jit(solution)/shard_map/ppermute | solution.py:236
  12.0 10.8 %collective-permute-start.2 = (bf16[256,256]{1,0:T(8,128)(2,1)S(1)}, bf16[256,256]{1,0:T(8,128)(2,1)S(1)}, u32[]{:S(2)}, u32[]{:S(2)}) collective-permute-start(bf16[256,256]{1,0:T(8,128)(2,1)S(1)} %get-tuple-element.38), channel_id=1, source_target_pairs={{0,121},{1,122},{2,123},{3,124},{4,125},{5,126},{6,127},{7,120},{8... | collective-permute-start | bytes 393224 | tf_op jit(solution)/shard_map/ppermute | solution.py:237
  24.2 9.2 %collective-permute-start.3 = (bf16[2,256,256]{2,1,0:T(8,128)(2,1)S(1)}, bf16[2,256,256]{2,1,0:T(8,128)(2,1)S(1)}, u32[]{:S(2)}, u32[]{:S(2)}) collective-permute-start(bf16[2,256,256]{2,1,0:T(8,128)(2,1)S(1)} %get-tuple-element.43), channel_id=1, source_target_pairs={{121,0},{122,1},{123,2},{124,3},{125,4},{126,5},{127,6},{120,7},{1... | collective-permute-start | bytes 786440 | tf_op jit(solution)/shard_map/ppermute | solution.py:259

commit v3 on v2

v3 whole, which is shorter than its diff:
```python
import functools
import math

import jax
import jax.numpy as jnp
from jax import lax
from jax.experimental import pallas as pl
from jax.experimental.pallas import tpu as pltpu
from jax.sharding import PartitionSpec as P


rate_users = 0.1
rate_items = 0.1
weight_decay = 0.02
adagrad_eps = 1e-08

CHUNK = 1024
F32 = jnp.float32
BF16 = jnp.bfloat16
TILE = 16
PIECES = 8


def dot(left, right, dims):
    return lax.dot_general(left, right, (dims, ((), ())), preferred_element_type=F32)


def place_slots(slots, dense, mask, ids_u, ids_i, counts, stratum, row, item_blocks):
    mask[...] = jnp.zeros(mask.shape, BF16)
    for n in range(slots.shape[0]):
        code = ids_u[0, 0, stratum, n] * item_blocks + ids_i[0, 0, stratum, n]
        live = jnp.where(n < counts[0, stratum, row], 1.0, 0.0)
        mask[code] = jnp.full(mask.shape[1:], live, F32).astype(BF16)
        dense[code] = slots[n]


def id_copies(ids_u, ids_i, counts, ids_u_s, ids_i_s, counts_s, row, sems):
    here = pl.ds(row, 1)
    return [
        pltpu.make_async_copy(ids_u.at[here], ids_u_s, sems.at[0]),
        pltpu.make_async_copy(ids_i.at[here], ids_i_s, sems.at[1]),
        pltpu.make_async_copy(counts, counts_s, sems.at[2]),
    ]


def load_kernel(block, users, items, accum, ratings, ids_u, ids_i, counts,
                users_out, items_out, accum_out, later_out, dense, mask,
                slots, ids_u_s, ids_i_s, counts_s, id_sems, data_sems):
    row = lax.axis_index("au")
    small = id_copies(ids_u, ids_i, counts, ids_u_s, ids_i_s, counts_s, row, id_sems)
    large = [
        pltpu.make_async_copy(ratings.at[0, 0, 0], slots, data_sems.at[0]),
        pltpu.make_async_copy(ratings.at[0, 0, 1], later_out, data_sems.at[1]),
        pltpu.make_async_copy(items, items_out, data_sems.at[2]),
        pltpu.make_async_copy(accum, accum_out, data_sems.at[3]),
    ]
    piece = users.shape[0] // PIECES
    for at in range(PIECES):
        span = pl.ds(at * piece, piece)
        large.append(
            pltpu.make_async_copy(users.at[span], users_out.at[span], data_sems.at[4 + at])
        )
    for copy in small + large:
        copy.start()
    for copy in small + large[:1]:
        copy.wait()
    place_slots(slots, dense, mask, ids_u_s, ids_i_s, counts_s, 0, row, items.shape[0] // block)
    for copy in large[1:]:
        copy.wait()


def residual_chunk(predicted, dense, mask, first, block, out):
    rows, cols = predicted.shape
    for r in range(rows // block):
        for c in range(cols // block):
            code = (first // block + r) * (cols // block) + c
            part = predicted[r * block : (r + 1) * block, c * block : (c + 1) * block]
            value = (dense[code].astype(F32) - part).astype(BF16)
            flag = jnp.concatenate([mask[code]] * (block // TILE), axis=0)
            out[pl.ds(first + r * block, block), pl.ds(c * block, block)] = jnp.where(
                flag != 0, value, jnp.zeros_like(value)
            )


def sgd_step(source, scaled, dense, mask, resid, copies, user_out, block):
    rows = source.shape[0]
    for c in range(rows // CHUNK):
        span = pl.ds(c * CHUNK, CHUNK)
        user = source[span, :]
        user_copy = user.astype(BF16)
        copies[span, :] = user_copy
        predicted = dot(user_copy, scaled, ((1,), (1,)))
        residual_chunk(predicted, dense, mask, c * CHUNK, block, resid)
        if user_out is not None:
            user_out[span, :] = user_step(user, dot(resid[span, :], scaled, ((1,), (0,))))
    return dot(resid[...], copies[...], ((0,), (0,)))


def user_step(user, scaled_total):
    return (1.0 - rate_users * weight_decay) * user + rate_users * scaled_total


def adagrad(item, acc, grad):
    acc = acc + grad * grad
    return item - rate_items * grad / jnp.sqrt(acc + adagrad_eps), acc


def item_step(item, acc, total):
    return adagrad(item, acc, gradient(item, total))


def scale(item):
    return item.astype(BF16) * BF16(1.0 / math.sqrt(item.shape[-1]))


def user_update(users, resid, scaled, user_out):
    for c in range(users.shape[0] // CHUNK):
        span = pl.ds(c * CHUNK, CHUNK)
        user_out[span, :] = user_step(users[span, :], dot(resid[span, :], scaled[...], ((1,), (0,))))


def first_kernel(block, users, items, accum, dense, mask,
                 user_out, resid, scaled_out, item_out, acc_out, item_send, acc_send, copies):
    item = items[...]
    total = sgd_step(users, scale(item), dense, mask, resid, copies, user_out, block)
    item, acc = item_step(item, accum[...], total)
    scaled = scale(item)
    scaled_out[...] = scaled
    total = sgd_step(user_out, scaled, dense, mask, resid, copies, None, block)
    item, acc = item_step(item, acc, total)
    item_out[...] = item
    acc_out[...] = acc
    item_send[...] = item.astype(BF16)
    acc_send[...] = acc.astype(BF16)


def turn_kernel(item_blocks, users, resid, scaled, later, ids_u, ids_i, counts,
                user_out, dense, mask, ids_u_s, ids_i_s, counts_s, id_sems):
    row = lax.rem(lax.axis_index("au") + 1, lax.axis_size("au"))
    small = id_copies(ids_u, ids_i, counts, ids_u_s, ids_i_s, counts_s, row, id_sems)
    for copy in small:
        copy.start()
    user_update(users, resid, scaled, user_out)
    for copy in small:
        copy.wait()
    place_slots(later, dense, mask, ids_u_s, ids_i_s, counts_s, 1, row, item_blocks)


def gradient(item, total):
    return weight_decay * item - (1.0 / math.sqrt(item.shape[-1])) * total


def second_kernel(block, users, items, dense, mask, user_out, grad_out, grad_send, resid, copies):
    item = items[...].astype(F32)
    total = sgd_step(users, scale(item), dense, mask, resid, copies, user_out, block)
    grad = gradient(item, total)
    grad_out[...] = grad
    grad_send[...] = grad.astype(BF16)


def third_kernel(block, users, items, accum, grad, dense, mask,
                 resid, scaled_out, grad_send, copies):
    item, _ = adagrad(items[...].astype(F32), accum[...].astype(F32), grad[...])
    scaled = scale(item)
    scaled_out[...] = scaled
    total = sgd_step(users, scaled, dense, mask, resid, copies, None, block)
    grad_send[...] = gradient(item, total).astype(BF16)


def vmem(count):
    return [pl.BlockSpec(memory_space=pltpu.VMEM)] * count


def hbm(count):
    return [pl.BlockSpec(memory_space=pltpu.HBM)] * count


def call(body, in_specs, outs, scratch, args):
    return pl.pallas_call(
        body,
        out_shape=tuple(jax.ShapeDtypeStruct(shape, dtype) for shape, dtype in outs),
        in_specs=in_specs,
        out_specs=tuple(vmem(len(outs))),
        scratch_shapes=scratch,
        compiler_params=pltpu.CompilerParams(vmem_limit_bytes=24 << 20),
    )(*args)


def in_hbm(*values):
    return [pltpu.with_memory_space_constraint(value, pltpu.HBM) for value in values]


def whole(users, items, accum, ratings, block_users, block_items, block_counts):
    rows, width = users.shape
    cols = items.shape[0]
    strata, slots, block = ratings.shape[2], ratings.shape[3], ratings.shape[-1]
    counts = jnp.transpose(block_counts, (1, 2, 0))
    n_au, n_ia = lax.axis_size("au"), lax.axis_size("ia")
    user_shape, item_shape = ((rows, width), F32), ((cols, width), F32)
    resid_shape, copy_shape = ((rows, cols), BF16), ((cols, width), BF16)
    slots_shape = ((slots, block, block), BF16)
    dense_shape = (((rows // block) * (cols // block), block, block), BF16)
    mask_shape = (((rows // block) * (cols // block), TILE, block), BF16)
    user_copies = pltpu.VMEM((rows, width), BF16)
    dma = pltpu.SemaphoreType.DMA
    ids_smem = pltpu.SMEM((1, 1, strata, slots), jnp.int32)

    def at(a, i):
        return (a % n_au) * n_ia + i % n_ia

    places = [(a, i) for a in range(n_au) for i in range(n_ia)]
    out_pairs = [(at(a, i), at(a - 1, i + 1)) for a, i in places]
    back_pairs = [(target, source) for source, target in out_pairs]

    tables = [ids_smem, ids_smem, pltpu.SMEM(counts.shape, jnp.int32), dma((3,))]
    user, item, acc, later, dense, mask = call(
        functools.partial(load_kernel, block),
        hbm(7),
        (user_shape, item_shape, item_shape, slots_shape, dense_shape, mask_shape),
        [pltpu.VMEM(*slots_shape)] + tables + [dma((4 + PIECES,))],
        in_hbm(users, items, accum, ratings, block_users, block_items, counts),
    )
    later = lax.ppermute(later, "au", [(a, (a - 1) % n_au) for a in range(n_au)])
    user, resid, scaled, item_mid, acc_mid, item_sent, acc_sent = call(
        functools.partial(first_kernel, block),
        vmem(5),
        (user_shape, resid_shape, copy_shape, item_shape, item_shape, copy_shape, copy_shape),
        [user_copies],
        (user, item, acc, dense, mask),
    )
    item_here = lax.ppermute(item_sent, ("au", "ia"), out_pairs)
    acc_here = lax.ppermute(acc_sent, ("au", "ia"), out_pairs)
    user, dense, mask = call(
        functools.partial(turn_kernel, cols // block),
        vmem(4) + hbm(3),
        (user_shape, dense_shape, mask_shape),
        tables,
        [user, resid, scaled, later] + in_hbm(block_users, block_items, counts),
    )
    user, grad, grad_sent = call(
        functools.partial(second_kernel, block),
        vmem(4),
        (user_shape, item_shape, copy_shape),
        [pltpu.VMEM(*resid_shape), user_copies],
        (user, item_here, dense, mask),
    )
    home = lax.ppermute(grad_sent, ("au", "ia"), back_pairs)
    resid, scaled, grad_sent = call(
        functools.partial(third_kernel, block),
        vmem(6),
        (resid_shape, copy_shape, copy_shape),
        [user_copies],
        (user, item_here, acc_here, grad, dense, mask),
    )
    home_last = lax.ppermute(grad_sent, ("au", "ia"), back_pairs)
    (user,) = call(user_update, vmem(3), (user_shape,), [], (user, resid, scaled))
    new_items, new_accum = adagrad(item_mid, acc_mid, home.astype(F32))
    new_items, new_accum = adagrad(new_items, new_accum, home_last.astype(F32))
    return user, new_items, new_accum


def solution(mesh):
    return jax.shard_map(
        whole,
        mesh=mesh,
        in_specs=(
            P(("au", "ia"), None),
            P(("au", "ia"), None),
            P(("au", "ia"), None),
            P("au", "ia", None, None, None, None),
            P(None, "ia", None, None),
            P(None, "ia", None, None),
            P(None, "ia", None),
        ),
        out_specs=(P(("au", "ia"), None), P(("au", "ia"), None), P(("au", "ia"), None)),
        check_vma=False,
    )
```

time: 34.4 us -> 34.2 us (level)
  Pallas kernels: 10.6 us -> 9.98 us
  waiting for transfers between devices: 13.7 us -> 14.2 us
    sub x0 -> x1, other arithmetic: none -> 0.92 us  [adagrad(): return (item - rate_items * grad / jnp.sqrt(acc + adagrad_eps), acc)]
    add x1 -> x0, other arithmetic: 0.84 us -> none  [local(): return (user, item_mid + home[0].astype(F32), acc_mid + home[1].astype(F32))]
    pallas_call x6, Pallas kernels: 10.6 us -> 9.98 us  [call(): pl.pallas_call(body, out_shape=tuple((jax.ShapeDtypeStruct(shape, dtype)...]
    ppermute x4 -> x5, waiting for transfers between devices: 13.7 us -> 14.2 us  [the longest x1 5.51 us: whole(): home_last = lax.ppermute(grad_sent, ('au', 'ia'), back_pairs)]
    ppermute x4 -> x5, starting transfers between devices: 8.49 us -> 8.26 us  [the longest x1 3.73 us: whole(): lax.ppermute(later, 'au', [(a, (a - 1) % n_au) for a in range(n_au)])]
  transfers between devices with their start and end apart: 4 -> 5, of which waited for: 4 -> 5; matrix products, arithmetic and copies ran while one was open for 0% -> 0% of each run, Pallas kernels for 20% -> 19%
where the time goes in v3:
time: 34.2 us; the launch traced here: 34 us
  waiting for transfers between devices  14.2 us (42%)
  Pallas kernels  9.98 us (29%)
  starting transfers between devices  8.26 us (24%)
  other arithmetic  0.92 us (3%)
  between operations  0.67 us (2%)
    pallas_call x6, Pallas kernels, call(): pl.pallas_call(body, out_shape=tuple((jax.ShapeDtypeStruct(shape, dtype)...  9.98 us
    ppermute x1, waiting for transfers between devices, whole(): home_last = lax.ppermute(grad_sent, ('au', 'ia'), back_pairs)  5.51 us
    ppermute x1, waiting for transfers between devices, whole(): acc_here = lax.ppermute(acc_sent, ('au', 'ia'), out_pairs)  4.13 us
    ppermute x1, starting transfers between devices, whole(): lax.ppermute(later, 'au', [(a, (a - 1) % n_au) for a in range(n_au)])  3.73 us
    ppermute x1, waiting for transfers between devices, whole(): item_here = lax.ppermute(item_sent, ('au', 'ia'), out_pairs)  2.97 us
    ppermute x1, starting transfers between devices, whole(): item_here = lax.ppermute(item_sent, ('au', 'ia'), out_pairs)  2.87 us
    ppermute x1, waiting for transfers between devices, whole(): home = lax.ppermute(grad_sent, ('au', 'ia'), back_pairs)  1.4 us
    ppermute x1, starting transfers between devices, whole(): acc_here = lax.ppermute(acc_sent, ('au', 'ia'), out_pairs)  1.19 us
  transfers between devices with their start and end apart: 5, of which 5 were waited for; matrix products, arithmetic and copies ran while one was open for 0% of the time, Pallas kernels for 19%

profile of v3, /device:TPU:0, one launch (start us, length us, event | category | flops | bytes accessed | tf_op | source)
XLA Modules:
  0.0 34.0 jit_solution(16213970356659365927)
XLA Ops:
  0.6 2.1 %shard_map.94 = (f32[2048,256]{1,0:T(8,128)S(1)}, f32[256,256]{1,0:T(8,128)S(1)}, f32[256,256]{1,0:T(8,128)S(1)}, bf16[16,128,128]{2,1,0:T(8,128)(2,1)S(1)}, bf1...) custom-call(f32[2048,256]{1,0:T(8,128)} %users.1, f32[256,256]{1,0:T(8,128)} %items.1, f32[256,256]{1,0:T(8,128)} %accum.1, ...), custom_call_target="tpu_custom_call" | custom-call | tf_op jit(solution)/shard_map/pallas_call | solution.py:179
  2.7 3.7 %collective-permute-start = (bf16[16,128,128]{2,1,0:T(8,128)(2,1)S(1)}, bf16[16,128,128]{2,1,0:T(8,128)(2,1)S(1)}, u32[]{:S(2)}, u32[]{:S(2)}) collective-permute-start(bf16[16,128,128]{2,1,0:T(8,128)(2,1)S(1)} %get-tuple-element.33), channel_id=1, source_target_pairs={{0,120},{8,0},{16,8},{24,16},{32,24},{40,32},{48,40},{56,48},{64,5... | collective-permute-start | bytes 1572872 | tf_op jit(solution)/shard_map/ppermute | solution.py:223
  6.5 2.5 %shard_map.95 = (f32[2048,256]{1,0:T(8,128)S(1)}, bf16[2048,256]{1,0:T(8,128)(2,1)S(1)}, bf16[256,256]{1,0:T(8,128)(2,1)S(1)}, f32[256,256]{1,0:T(8,128)S(1)}, f...) custom-call(f32[2048,256]{1,0:T(8,128)S(1)} %get-tuple-element.25.users, ...), custom_call_target="tpu_custom_call" | custom-call | tf_op jit(solution)/shard_map/pallas_call | solution.py:179
  9.0 2.9 %collective-permute-start.1 = (bf16[256,256]{1,0:T(8,128)(2,1)S(1)}, bf16[256,256]{1,0:T(8,128)(2,1)S(1)}, u32[]{:S(2)}, u32[]{:S(2)}) collective-permute-start(bf16[256,256]{1,0:T(8,128)(2,1)S(1)} %get-tuple-element.35), channel_id=1, source_target_pairs={{0,121},{1,122},{2,123},{3,124},{4,125},{5,126},{6,127},{7,120},{8... | collective-permute-start | bytes 393224 | tf_op jit(solution)/shard_map/ppermute | solution.py:231
  11.8 1.2 %collective-permute-start.2 = (bf16[256,256]{1,0:T(8,128)(2,1)S(1)}, bf16[256,256]{1,0:T(8,128)(2,1)S(1)}, u32[]{:S(2)}, u32[]{:S(2)}) collective-permute-start(bf16[256,256]{1,0:T(8,128)(2,1)S(1)} %get-tuple-element.39), channel_id=1, source_target_pairs={{0,121},{1,122},{2,123},{3,124},{4,125},{5,126},{6,127},{7,120},{8... | collective-permute-start | bytes 393224 | tf_op jit(solution)/shard_map/ppermute | solution.py:232
  13.0 0.2 collective-permute-done.later
  13.2 1.2 %shard_map.96 = (f32[2048,256]{1,0:T(8,128)S(1)}, bf16[32,128,128]{2,1,0:T(8,128)(2,1)S(1)}, bf16[32,16,128]{2,1,0:T(8,128)(2,1)S(1)}) custom-call(f32[2048,256]{1,0:T(8,128)S(1)} %get-tuple-element.30.users, bf16[2048,256]{1,0:T(8,128)(2,1)S(1)} %get-tuple-element.31.resid, bf16[256,256]{1,0:T(8,128)(2,1)S(1)} %get-tuple-element.32.scaled, ...), custom_call_target="tpu_custom_call" | custom-call | tf_op jit(solution)/shard_map/pallas_call | solution.py:179
  14.4 3.0 %collective-permute-done.1.items = bf16[256,256]{1,0:T(8,128)(2,1)S(1)} collective-permute-done((bf16[256,256]{1,0:T(8,128)(2,1)S(1)}, bf16[256,256]{1,0:T(8,128)(2,1)S(1)}, u32[]{:S(2)}, u32[]{:S(2)}) %collective-permute-start.1) | collective-permute-done | bytes 131104 | tf_op jit(solution)/shard_map/ppermute | solution.py:231
  17.4 1.1 %shard_map.97 = (f32[2048,256]{1,0:T(8,128)S(1)}, f32[256,256]{1,0:T(8,128)S(1)}, bf16[256,256]{1,0:T(8,128)(2,1)S(1)}) custom-call(f32[2048,256]{1,0:T(8,128)S(1)} %get-tuple-element.34.users, bf16[256,256]{1,0:T(8,128)(2,1)S(1)} %collective-permute-done.1.items, bf16[32,128,128]{2,1,0:T(8,128)(2,1)S(1)} %get-tuple-element.36.dense, ...), custom_call_target="tpu_custom_call" | custom-call | tf_op jit(solution)/shard_map/pallas_call | solution.py:179
  18.5 4.1 %collective-permute-done.2.accum = bf16[256,256]{1,0:T(8,128)(2,1)S(1)} collective-permute-done((bf16[256,256]{1,0:T(8,128)(2,1)S(1)}, bf16[256,256]{1,0:T(8,128)(2,1)S(1)}, u32[]{:S(2)}, u32[]{:S(2)}) %collective-permute-start.2) | collective-permute-done | bytes 131104 | tf_op jit(solution)/shard_map/ppermute | solution.py:232
  22.6 1.3 %shard_map.98 = (bf16[2048,256]{1,0:T(8,128)(2,1)S(1)}, bf16[256,256]{1,0:T(8,128)(2,1)S(1)}, bf16[256,256]{1,0:T(8,128)(2,1)S(1)}) custom-call(f32[2048,256]{1,0:T(8,128)S(1)} %get-tuple-element.38.users, bf16[256,256]{1,0:T(8,128)(2,1)S(1)} %collective-permute-done.1.items, bf16[256,256]{1,0:T(8,128)(2,1)S(1)} %collective-permute-done.2.accum, ...), custom_call_target="tpu_custom_call" | custom-call | tf_op jit(solution)/shard_map/pallas_call | solution.py:179
  23.9 0.4 %collective-permute-start.4 = (bf16[256,256]{1,0:T(8,128)(2,1)S(1)}, bf16[256,256]{1,0:T(8,128)(2,1)S(1)}, u32[]{:S(2)}, u32[]{:S(2)}) collective-permute-start(bf16[256,256]{1,0:T(8,128)(2,1)S(1)} %get-tuple-element.46), channel_id=1, source_target_pairs={{121,0},{122,1},{123,2},{124,3},{125,4},{126,5},{127,6},{120,7},{1... | collective-permute-start | bytes 393224 | tf_op jit(solution)/shard_map/ppermute | solution.py:255
  24.3 0.1 collective-permute-start.3
  24.4 1.8 %shard_map.99 = f32[2048,256]{1,0:T(8,128)} custom-call(f32[2048,256]{1,0:T(8,128)S(1)} %get-tuple-element.38.users, bf16[2048,256]{1,0:T(8,128)(2,1)S(1)} %get-tuple-element.41.resid, bf16[256,256]{1,0:T(8,128)(2,1)S(1)} %get-tuple-element.42.scaled), custom_call_target="tpu_custom_call" | custom-call | tf_op jit(solution)/shard_map/pallas_call | solution.py:179
  26.2 5.5 %collective-permute-done.4 = bf16[256,256]{1,0:T(8,128)(2,1)S(1)} collective-permute-done((bf16[256,256]{1,0:T(8,128)(2,1)S(1)}, bf16[256,256]{1,0:T(8,128)(2,1)S(1)}, u32[]{:S(2)}, u32[]{:S(2)}) %collective-permute-start.4) | collective-permute-done | bytes 131104 | tf_op jit(solution)/shard_map/ppermute | solution.py:255
  31.7 1.4 %collective-permute-done.3 = bf16[256,256]{1,0:T(8,128)(2,1)S(1)} collective-permute-done((bf16[256,256]{1,0:T(8,128)(2,1)S(1)}, bf16[256,256]{1,0:T(8,128)(2,1)S(1)}, u32[]{:S(2)}, u32[]{:S(2)}) %collective-permute-start.3) | collective-permute-done | bytes 131104 | tf_op jit(solution)/shard_map/ppermute | solution.py:247
  33.1 0.9 %fusion.2 = (f32[256,256]{1,0:T(8,128)}, f32[256,256]{1,0:T(8,128)}) fusion(f32[256,256]{1,0:T(8,128)S(1)} %get-tuple-element.43, bf16[256,256]{1,0:T(8,128)(2,1)S(1)} %collective-permute-done.3, bf16[256,256]{1,0:T(8,128)(2,1)S(1)} %collective-permute-done.4, f32[256,256]{1,0:T(8,128)S(1)} %get-tuple-element.45), kind=kLoop, calls=%fused_computation.6 | loop fusion | flops 917504 | bytes 1310720 | tf_op jit(solution)/shard_map/sub | solution.py:105
Async XLA Ops:
  2.7 10.4 %collective-permute-start = (bf16[16,128,128]{2,1,0:T(8,128)(2,1)S(1)}, bf16[16,128,128]{2,1,0:T(8,128)(2,1)S(1)}, u32[]{:S(2)}, u32[]{:S(2)}) collective-permute-start(bf16[16,128,128]{2,1,0:T(8,128)(2,1)S(1)} %get-tuple-element.33), channel_id=1, source_target_pairs={{0,120},{8,0},{16,8},{24,16},{32,24},{40,32},{48,40},{56,48},{64,5... | collective-permute-start | bytes 1572872 | tf_op jit(solution)/shard_map/ppermute | solution.py:223
  9.0 8.4 %collective-permute-start.1 = (bf16[256,256]{1,0:T(8,128)(2,1)S(1)}, bf16[256,256]{1,0:T(8,128)(2,1)S(1)}, u32[]{:S(2)}, u32[]{:S(2)}) collective-permute-start(bf16[256,256]{1,0:T(8,128)(2,1)S(1)} %get-tuple-element.35), channel_id=1, source_target_pairs={{0,121},{1,122},{2,123},{3,124},{4,125},{5,126},{6,127},{7,120},{8... | collective-permute-start | bytes 393224 | tf_op jit(solution)/shard_map/ppermute | solution.py:231
  11.8 10.8 %collective-permute-start.2 = (bf16[256,256]{1,0:T(8,128)(2,1)S(1)}, bf16[256,256]{1,0:T(8,128)(2,1)S(1)}, u32[]{:S(2)}, u32[]{:S(2)}) collective-permute-start(bf16[256,256]{1,0:T(8,128)(2,1)S(1)} %get-tuple-element.39), channel_id=1, source_target_pairs={{0,121},{1,122},{2,123},{3,124},{4,125},{5,126},{6,127},{7,120},{8... | collective-permute-start | bytes 393224 | tf_op jit(solution)/shard_map/ppermute | solution.py:232
  23.9 7.8 %collective-permute-start.4 = (bf16[256,256]{1,0:T(8,128)(2,1)S(1)}, bf16[256,256]{1,0:T(8,128)(2,1)S(1)}, u32[]{:S(2)}, u32[]{:S(2)}) collective-permute-start(bf16[256,256]{1,0:T(8,128)(2,1)S(1)} %get-tuple-element.46), channel_id=1, source_target_pairs={{121,0},{122,1},{123,2},{124,3},{125,4},{126,5},{127,6},{120,7},{1... | collective-permute-start | bytes 393224 | tf_op jit(solution)/shard_map/ppermute | solution.py:255
  24.3 8.8 %collective-permute-start.3 = (bf16[256,256]{1,0:T(8,128)(2,1)S(1)}, bf16[256,256]{1,0:T(8,128)(2,1)S(1)}, u32[]{:S(2)}, u32[]{:S(2)}) collective-permute-start(bf16[256,256]{1,0:T(8,128)(2,1)S(1)} %get-tuple-element.44), channel_id=1, source_target_pairs={{121,0},{122,1},{123,2},{124,3},{125,4},{126,5},{127,6},{120,7},{1... | collective-permute-start | bytes 393224 | tf_op jit(solution)/shard_map/ppermute | solution.py:247

commit v4 on v3

--- a/solution.py
+++ b/solution.py
@@ -134,8 +134,8 @@
     acc_send[...] = acc.astype(BF16)
 
 
-def turn_kernel(item_blocks, users, resid, scaled, later, ids_u, ids_i, counts,
-                user_out, dense, mask, ids_u_s, ids_i_s, counts_s, id_sems):
+def turn_kernel(item_blocks, users, resid, scaled, ids_u, ids_i, counts,
+                user_out, mask, codes, ids_u_s, ids_i_s, counts_s, id_sems):
     row = lax.rem(lax.axis_index("au") + 1, lax.axis_size("au"))
     small = id_copies(ids_u, ids_i, counts, ids_u_s, ids_i_s, counts_s, row, id_sems)
     for copy in small:
@@ -143,7 +143,17 @@
     user_update(users, resid, scaled, user_out)
     for copy in small:
         copy.wait()
-    place_slots(later, dense, mask, ids_u_s, ids_i_s, counts_s, 1, row, item_blocks)
+    mask[...] = jnp.zeros(mask.shape, BF16)
+    for n in range(codes.shape[0]):
+        code = ids_u_s[0, 0, 1, n] * item_blocks + ids_i_s[0, 0, 1, n]
+        live = jnp.where(n < counts_s[0, 1, row], 1.0, 0.0)
+        mask[code] = jnp.full(mask.shape[1:], live, F32).astype(BF16)
+        codes[n] = code
+
+
+def place_kernel(later, codes, dense):
+    for n in range(later.shape[0]):
+        dense[codes[n]] = later[n]
 
 
 def gradient(item, total):
@@ -175,12 +185,12 @@
     return [pl.BlockSpec(memory_space=pltpu.HBM)] * count
 
 
-def call(body, in_specs, outs, scratch, args):
+def call(body, in_specs, outs, scratch, args, out_specs=None):
     return pl.pallas_call(
         body,
         out_shape=tuple(jax.ShapeDtypeStruct(shape, dtype) for shape, dtype in outs),
         in_specs=in_specs,
-        out_specs=tuple(vmem(len(outs))),
+        out_specs=tuple(out_specs or vmem(len(outs))),
         scratch_shapes=scratch,
         compiler_params=pltpu.CompilerParams(vmem_limit_bytes=24 << 20),
     )(*args)
@@ -230,13 +240,16 @@
     )
     item_here = lax.ppermute(item_sent, ("au", "ia"), out_pairs)
     acc_here = lax.ppermute(acc_sent, ("au", "ia"), out_pairs)
-    user, dense, mask = call(
+    smem = [pl.BlockSpec(memory_space=pltpu.SMEM)]
+    user, mask, codes = call(
         functools.partial(turn_kernel, cols // block),
-        vmem(4) + hbm(3),
-        (user_shape, dense_shape, mask_shape),
+        vmem(3) + hbm(3),
+        (user_shape, mask_shape, ((slots,), jnp.int32)),
         tables,
-        [user, resid, scaled, later] + in_hbm(block_users, block_items, counts),
-    )
+        [user, resid, scaled] + in_hbm(block_users, block_items, counts),
+        vmem(2) + smem,
+    )
+    (dense,) = call(place_kernel, vmem(1) + smem, (dense_shape,), [], (later, codes))
     user, grad, grad_sent = call(
         functools.partial(second_kernel, block),
         vmem(4),

time: 34.2 us -> 34.2 us (level)
  Pallas kernels: 9.98 us -> 11.2 us
  waiting for transfers between devices: 14.2 us -> 13.3 us
    pallas_call x6 -> x7, Pallas kernels: 9.98 us -> 11.2 us  [call(): pl.pallas_call(body, out_shape=tuple((jax.ShapeDtypeStruct(shape, dtype)...]
    ppermute x1, waiting for transfers between devices: 2.97 us -> 1.95 us  [whole(): item_here = lax.ppermute(item_sent, ('au', 'ia'), out_pairs)]
  transfers between devices with their start and end apart: 5 -> 5, of which waited for: 5 -> 4; matrix products, arithmetic and copies ran while one was open for 0% -> 0% of each run, Pallas kernels for 19% -> 23%
where the time goes in v4:
time: 34.2 us; the launch traced here: 34.1 us
  waiting for transfers between devices  13.3 us (39%)
  Pallas kernels  11.2 us (33%)
  starting transfers between devices  7.94 us (23%)
  other arithmetic  0.92 us (3%)
  between operations  0.7 us (2%)
    pallas_call x7, Pallas kernels, call(): pl.pallas_call(body, out_shape=tuple((jax.ShapeDtypeStruct(shape, dtype)...  11.2 us
    ppermute x1, waiting for transfers between devices, whole(): home_last = lax.ppermute(grad_sent, ('au', 'ia'), back_pairs)  5.82 us
    ppermute x1, waiting for transfers between devices, whole(): acc_here = lax.ppermute(acc_sent, ('au', 'ia'), out_pairs)  4.13 us
    ppermute x1, starting transfers between devices, whole(): lax.ppermute(later, 'au', [(a, (a - 1) % n_au) for a in range(n_au)])  3.73 us
    ppermute x1, starting transfers between devices, whole(): item_here = lax.ppermute(item_sent, ('au', 'ia'), out_pairs)  2.87 us
    ppermute x1, waiting for transfers between devices, whole(): item_here = lax.ppermute(item_sent, ('au', 'ia'), out_pairs)  1.95 us
    ppermute x1, waiting for transfers between devices, whole(): home = lax.ppermute(grad_sent, ('au', 'ia'), back_pairs)  1.4 us
    ppermute x1, starting transfers between devices, whole(): acc_here = lax.ppermute(acc_sent, ('au', 'ia'), out_pairs)  1.19 us
  transfers between devices with their start and end apart: 5, of which 4 were waited for; matrix products, arithmetic and copies ran while one was open for 0% of the time, Pallas kernels for 23%

profile of v4, /device:TPU:0, one launch (start us, length us, event | category | flops | bytes accessed | tf_op | source)
XLA Modules:
  0.0 34.1 jit_solution(4506207011567513153)
XLA Ops:
  0.6 2.1 %shard_map.94 = (f32[2048,256]{1,0:T(8,128)S(1)}, f32[256,256]{1,0:T(8,128)S(1)}, f32[256,256]{1,0:T(8,128)S(1)}, bf16[16,128,128]{2,1,0:T(8,128)(2,1)S(1)}, bf1...) custom-call(f32[2048,256]{1,0:T(8,128)} %users.1, f32[256,256]{1,0:T(8,128)} %items.1, f32[256,256]{1,0:T(8,128)} %accum.1, ...), custom_call_target="tpu_custom_call" | custom-call | tf_op jit(solution)/shard_map/pallas_call | solution.py:189
  2.7 3.7 %collective-permute-start.1 = (bf16[16,128,128]{2,1,0:T(8,128)(2,1)S(1)}, bf16[16,128,128]{2,1,0:T(8,128)(2,1)S(1)}, u32[]{:S(2)}, u32[]{:S(2)}) collective-permute-start(bf16[16,128,128]{2,1,0:T(8,128)(2,1)S(1)} %get-tuple-element.35), channel_id=1, source_target_pairs={{0,120},{8,0},{16,8},{24,16},{32,24},{40,32},{48,40},{56,48},{64,5... | collective-permute-start | bytes 1572872 | tf_op jit(solution)/shard_map/ppermute | solution.py:233
  6.5 2.5 %shard_map.95 = (f32[2048,256]{1,0:T(8,128)S(1)}, bf16[2048,256]{1,0:T(8,128)(2,1)S(1)}, bf16[256,256]{1,0:T(8,128)(2,1)S(1)}, f32[256,256]{1,0:T(8,128)S(1)}, f...) custom-call(f32[2048,256]{1,0:T(8,128)S(1)} %get-tuple-element.25.users, ...), custom_call_target="tpu_custom_call" | custom-call | tf_op jit(solution)/shard_map/pallas_call | solution.py:189
  9.0 2.9 %collective-permute-start = (bf16[256,256]{1,0:T(8,128)(2,1)S(1)}, bf16[256,256]{1,0:T(8,128)(2,1)S(1)}, u32[]{:S(2)}, u32[]{:S(2)}) collective-permute-start(bf16[256,256]{1,0:T(8,128)(2,1)S(1)} %get-tuple-element.34), channel_id=1, source_target_pairs={{0,121},{1,122},{2,123},{3,124},{4,125},{5,126},{6,127},{7,120},{8... | collective-permute-start | bytes 393224 | tf_op jit(solution)/shard_map/ppermute | solution.py:241
  11.9 1.2 %collective-permute-start.2 = (bf16[256,256]{1,0:T(8,128)(2,1)S(1)}, bf16[256,256]{1,0:T(8,128)(2,1)S(1)}, u32[]{:S(2)}, u32[]{:S(2)}) collective-permute-start(bf16[256,256]{1,0:T(8,128)(2,1)S(1)} %get-tuple-element.39), channel_id=1, source_target_pairs={{0,121},{1,122},{2,123},{3,124},{4,125},{5,126},{6,127},{7,120},{8... | collective-permute-start | bytes 393224 | tf_op jit(solution)/shard_map/ppermute | solution.py:242
  13.1 1.8 %shard_map.96 = (f32[2048,256]{1,0:T(8,128)S(1)}, bf16[32,16,128]{2,1,0:T(8,128)(2,1)S(1)}, s32[16]{0:T(128)S(1)}) custom-call(f32[2048,256]{1,0:T(8,128)S(1)} %get-tuple-element.30.users, bf16[2048,256]{1,0:T(8,128)(2,1)S(1)} %get-tuple-element.31.resid, bf16[256,256]{1,0:T(8,128)(2,1)S(1)} %get-tuple-element.32.scaled, s32[16,1,2,16]{3,2,1,0:T(2,128)} %ids_u.3, ...), custom_call_target="tpu_custom_call" | custom-call | tf_op jit(solution)/shard_map/pallas_call | solution.py:189
  14.9 0.0 collective-permute-done.1.later
  14.9 0.6 %shard_map.97.dense = bf16[32,128,128]{2,1,0:T(8,128)(2,1)S(1)} custom-call(bf16[16,128,128]{2,1,0:T(8,128)(2,1)S(1)} %collective-permute-done.1.later, s32[16]{0:T(128)S(1)} %get-tuple-element.36.codes), custom_call_target="tpu_custom_call" | custom-call | tf_op jit(solution)/shard_map/pallas_call | solution.py:189
  15.5 1.9 %collective-permute-done.items = bf16[256,256]{1,0:T(8,128)(2,1)S(1)} collective-permute-done((bf16[256,256]{1,0:T(8,128)(2,1)S(1)}, bf16[256,256]{1,0:T(8,128)(2,1)S(1)}, u32[]{:S(2)}, u32[]{:S(2)}) %collective-permute-start) | collective-permute-done | bytes 131104 | tf_op jit(solution)/shard_map/ppermute | solution.py:241
  17.4 1.1 %shard_map.98 = (f32[2048,256]{1,0:T(8,128)S(1)}, f32[256,256]{1,0:T(8,128)S(1)}, bf16[256,256]{1,0:T(8,128)(2,1)S(1)}) custom-call(f32[2048,256]{1,0:T(8,128)S(1)} %get-tuple-element.33.users, bf16[256,256]{1,0:T(8,128)(2,1)S(1)} %collective-permute-done.items, bf16[32,128,128]{2,1,0:T(8,128)(2,1)S(1)} %shard_map.97.dense, ...), custom_call_target="tpu_custom_call" | custom-call | tf_op jit(solution)/shard_map/pallas_call | solution.py:189
  18.6 4.1 %collective-permute-done.2.accum = bf16[256,256]{1,0:T(8,128)(2,1)S(1)} collective-permute-done((bf16[256,256]{1,0:T(8,128)(2,1)S(1)}, bf16[256,256]{1,0:T(8,128)(2,1)S(1)}, u32[]{:S(2)}, u32[]{:S(2)}) %collective-permute-start.2) | collective-permute-done | bytes 131104 | tf_op jit(solution)/shard_map/ppermute | solution.py:242
  22.7 1.3 %shard_map.99 = (bf16[2048,256]{1,0:T(8,128)(2,1)S(1)}, bf16[256,256]{1,0:T(8,128)(2,1)S(1)}, bf16[256,256]{1,0:T(8,128)(2,1)S(1)}) custom-call(f32[2048,256]{1,0:T(8,128)S(1)} %get-tuple-element.38.users, bf16[256,256]{1,0:T(8,128)(2,1)S(1)} %collective-permute-done.items, bf16[256,256]{1,0:T(8,128)(2,1)S(1)} %collective-permute-done.2.accum, ...), custom_call_target="tpu_custom_call" | custom-call | tf_op jit(solution)/shard_map/pallas_call | solution.py:189
  24.0 0.1 collective-permute-start.4
  24.0 0.1 collective-permute-start.3
  24.1 1.8 %shard_map.100 = f32[2048,256]{1,0:T(8,128)} custom-call(f32[2048,256]{1,0:T(8,128)S(1)} %get-tuple-element.38.users, bf16[2048,256]{1,0:T(8,128)(2,1)S(1)} %get-tuple-element.41.resid, bf16[256,256]{1,0:T(8,128)(2,1)S(1)} %get-tuple-element.42.scaled), custom_call_target="tpu_custom_call" | custom-call | tf_op jit(solution)/shard_map/pallas_call | solution.py:189
  25.9 5.8 %collective-permute-done.4 = bf16[256,256]{1,0:T(8,128)(2,1)S(1)} collective-permute-done((bf16[256,256]{1,0:T(8,128)(2,1)S(1)}, bf16[256,256]{1,0:T(8,128)(2,1)S(1)}, u32[]{:S(2)}, u32[]{:S(2)}) %collective-permute-start.4) | collective-permute-done | bytes 131104 | tf_op jit(solution)/shard_map/ppermute | solution.py:268
  31.7 1.4 %collective-permute-done.3 = bf16[256,256]{1,0:T(8,128)(2,1)S(1)} collective-permute-done((bf16[256,256]{1,0:T(8,128)(2,1)S(1)}, bf16[256,256]{1,0:T(8,128)(2,1)S(1)}, u32[]{:S(2)}, u32[]{:S(2)}) %collective-permute-start.3) | collective-permute-done | bytes 131104 | tf_op jit(solution)/shard_map/ppermute | solution.py:260
  33.2 0.9 %fusion.2 = (f32[256,256]{1,0:T(8,128)}, f32[256,256]{1,0:T(8,128)}) fusion(f32[256,256]{1,0:T(8,128)S(1)} %get-tuple-element.43, bf16[256,256]{1,0:T(8,128)(2,1)S(1)} %collective-permute-done.3, bf16[256,256]{1,0:T(8,128)(2,1)S(1)} %collective-permute-done.4, f32[256,256]{1,0:T(8,128)S(1)} %get-tuple-element.45), kind=kLoop, calls=%fused_computation.6 | loop fusion | flops 917504 | bytes 1310720 | tf_op jit(solution)/shard_map/sub | solution.py:105
Async XLA Ops:
  2.7 12.2 %collective-permute-start.1 = (bf16[16,128,128]{2,1,0:T(8,128)(2,1)S(1)}, bf16[16,128,128]{2,1,0:T(8,128)(2,1)S(1)}, u32[]{:S(2)}, u32[]{:S(2)}) collective-permute-start(bf16[16,128,128]{2,1,0:T(8,128)(2,1)S(1)} %get-tuple-element.35), channel_id=1, source_target_pairs={{0,120},{8,0},{16,8},{24,16},{32,24},{40,32},{48,40},{56,48},{64,5... | collective-permute-start | bytes 1572872 | tf_op jit(solution)/shard_map/ppermute | solution.py:233
  9.0 8.4 %collective-permute-start = (bf16[256,256]{1,0:T(8,128)(2,1)S(1)}, bf16[256,256]{1,0:T(8,128)(2,1)S(1)}, u32[]{:S(2)}, u32[]{:S(2)}) collective-permute-start(bf16[256,256]{1,0:T(8,128)(2,1)S(1)} %get-tuple-element.34), channel_id=1, source_target_pairs={{0,121},{1,122},{2,123},{3,124},{4,125},{5,126},{6,127},{7,120},{8... | collective-permute-start | bytes 393224 | tf_op jit(solution)/shard_map/ppermute | solution.py:241
  11.9 10.8 %collective-permute-start.2 = (bf16[256,256]{1,0:T(8,128)(2,1)S(1)}, bf16[256,256]{1,0:T(8,128)(2,1)S(1)}, u32[]{:S(2)}, u32[]{:S(2)}) collective-permute-start(bf16[256,256]{1,0:T(8,128)(2,1)S(1)} %get-tuple-element.39), channel_id=1, source_target_pairs={{0,121},{1,122},{2,123},{3,124},{4,125},{5,126},{6,127},{7,120},{8... | collective-permute-start | bytes 393224 | tf_op jit(solution)/shard_map/ppermute | solution.py:242
  24.0 7.8 %collective-permute-start.4 = (bf16[256,256]{1,0:T(8,128)(2,1)S(1)}, bf16[256,256]{1,0:T(8,128)(2,1)S(1)}, u32[]{:S(2)}, u32[]{:S(2)}) collective-permute-start(bf16[256,256]{1,0:T(8,128)(2,1)S(1)} %get-tuple-element.46), channel_id=1, source_target_pairs={{121,0},{122,1},{123,2},{124,3},{125,4},{126,5},{127,6},{120,7},{1... | collective-permute-start | bytes 393224 | tf_op jit(solution)/shard_map/ppermute | solution.py:268
  24.0 9.1 %collective-permute-start.3 = (bf16[256,256]{1,0:T(8,128)(2,1)S(1)}, bf16[256,256]{1,0:T(8,128)(2,1)S(1)}, u32[]{:S(2)}, u32[]{:S(2)}) collective-permute-start(bf16[256,256]{1,0:T(8,128)(2,1)S(1)} %get-tuple-element.44), channel_id=1, source_target_pairs={{121,0},{122,1},{123,2},{124,3},{125,4},{126,5},{127,6},{120,7},{1... | collective-permute-start | bytes 393224 | tf_op jit(solution)/shard_map/ppermute | solution.py:260

commit v5 on v4

--- a/solution.py
+++ b/solution.py
@@ -69,17 +69,25 @@
         copy.wait()
 
 
-def residual_chunk(predicted, dense, mask, first, block, out):
+def residual_chunk(predicted, dense, mask, first, block):
     rows, cols = predicted.shape
-    for r in range(rows // block):
-        for c in range(cols // block):
-            code = (first // block + r) * (cols // block) + c
-            part = predicted[r * block : (r + 1) * block, c * block : (c + 1) * block]
-            value = (dense[code].astype(F32) - part).astype(BF16)
-            flag = jnp.concatenate([mask[code]] * (block // TILE), axis=0)
-            out[pl.ds(first + r * block, block), pl.ds(c * block, block)] = jnp.where(
-                flag != 0, value, jnp.zeros_like(value)
-            )
+
+    def spread(piece):
+        item_blocks = cols // block
+        return jnp.concatenate(
+            [
+                jnp.concatenate(
+                    [piece((first // block + r) * item_blocks + c) for c in range(item_blocks)],
+                    axis=1,
+                )
+                for r in range(rows // block)
+            ],
+            axis=0,
+        )
+
+    value = (spread(lambda code: dense[code]).astype(F32) - predicted).astype(BF16)
+    live = spread(lambda code: jnp.concatenate([mask[code]] * (block // TILE), axis=0))
+    return jnp.where(live != 0, value, jnp.zeros_like(value))
 
 
 def sgd_step(source, scaled, dense, mask, resid, copies, user_out, block):
@@ -90,9 +98,10 @@
         user_copy = user.astype(BF16)
         copies[span, :] = user_copy
         predicted = dot(user_copy, scaled, ((1,), (1,)))
-        residual_chunk(predicted, dense, mask, c * CHUNK, block, resid)
+        here = residual_chunk(predicted, dense, mask, c * CHUNK, block)
+        resid[span, :] = here
         if user_out is not None:
-            user_out[span, :] = user_step(user, dot(resid[span, :], scaled, ((1,), (0,))))
+            user_out[span, :] = user_step(user, dot(here, scaled, ((1,), (0,))))
     return dot(resid[...], copies[...], ((0,), (0,)))
 
 

time: 34.2 us -> 33.7 us (0.985)
  Pallas kernels: 11.2 us -> 10.6 us
    pallas_call x7, Pallas kernels: 11.2 us -> 10.6 us  [call(): pl.pallas_call(body, out_shape=tuple((jax.ShapeDtypeStruct(shape, dtype)...]
  transfers between devices with their start and end apart: 5 -> 5, of which waited for: 4 -> 4; matrix products, arithmetic and copies ran while one was open for 0% -> 0% of each run, Pallas kernels for 23% -> 22%
where the time goes in v5:
time: 33.7 us; the launch traced here: 33.6 us
  waiting for transfers between devices  13.4 us (40%)
  Pallas kernels  10.6 us (31%)
  starting transfers between devices  7.94 us (24%)
  other arithmetic  0.92 us (3%)
  between operations  0.7 us (2%)
    pallas_call x7, Pallas kernels, call(): pl.pallas_call(body, out_shape=tuple((jax.ShapeDtypeStruct(shape, dtype)...  10.6 us
    ppermute x1, waiting for transfers between devices, whole(): home_last = lax.ppermute(grad_sent, ('au', 'ia'), back_pairs)  5.82 us
    ppermute x1, waiting for transfers between devices, whole(): acc_here = lax.ppermute(acc_sent, ('au', 'ia'), out_pairs)  4.01 us
    ppermute x1, starting transfers between devices, whole(): lax.ppermute(later, 'au', [(a, (a - 1) % n_au) for a in range(n_au)])  3.73 us
    ppermute x1, starting transfers between devices, whole(): item_here = lax.ppermute(item_sent, ('au', 'ia'), out_pairs)  2.87 us
    ppermute x1, waiting for transfers between devices, whole(): item_here = lax.ppermute(item_sent, ('au', 'ia'), out_pairs)  2.15 us
    ppermute x1, waiting for transfers between devices, whole(): home = lax.ppermute(grad_sent, ('au', 'ia'), back_pairs)  1.4 us
    ppermute x1, starting transfers between devices, whole(): acc_here = lax.ppermute(acc_sent, ('au', 'ia'), out_pairs)  1.19 us
  transfers between devices with their start and end apart: 5, of which 4 were waited for; matrix products, arithmetic and copies ran while one was open for 0% of the time, Pallas kernels for 22%

profile of v5, /device:TPU:0, one launch (start us, length us, event | category | flops | bytes accessed | tf_op | source)
XLA Modules:
  0.0 33.6 jit_solution(16761077137871281659)
XLA Ops:
  0.6 2.1 %shard_map.94 = (f32[2048,256]{1,0:T(8,128)S(1)}, f32[256,256]{1,0:T(8,128)S(1)}, f32[256,256]{1,0:T(8,128)S(1)}, bf16[16,128,128]{2,1,0:T(8,128)(2,1)S(1)}, bf1...) custom-call(f32[2048,256]{1,0:T(8,128)} %users.1, f32[256,256]{1,0:T(8,128)} %items.1, f32[256,256]{1,0:T(8,128)} %accum.1, ...), custom_call_target="tpu_custom_call" | custom-call | tf_op jit(solution)/shard_map/pallas_call | solution.py:198
  2.7 3.7 %collective-permute-start.1 = (bf16[16,128,128]{2,1,0:T(8,128)(2,1)S(1)}, bf16[16,128,128]{2,1,0:T(8,128)(2,1)S(1)}, u32[]{:S(2)}, u32[]{:S(2)}) collective-permute-start(bf16[16,128,128]{2,1,0:T(8,128)(2,1)S(1)} %get-tuple-element.35), channel_id=1, source_target_pairs={{0,120},{8,0},{16,8},{24,16},{32,24},{40,32},{48,40},{56,48},{64,5... | collective-permute-start | bytes 1572872 | tf_op jit(solution)/shard_map/ppermute | solution.py:242
  6.5 2.2 %shard_map.95 = (f32[2048,256]{1,0:T(8,128)S(1)}, bf16[2048,256]{1,0:T(8,128)(2,1)S(1)}, bf16[256,256]{1,0:T(8,128)(2,1)S(1)}, f32[256,256]{1,0:T(8,128)S(1)}, f...) custom-call(f32[2048,256]{1,0:T(8,128)S(1)} %get-tuple-element.25.users, ...), custom_call_target="tpu_custom_call" | custom-call | tf_op jit(solution)/shard_map/pallas_call | solution.py:198
  8.7 2.9 %collective-permute-start = (bf16[256,256]{1,0:T(8,128)(2,1)S(1)}, bf16[256,256]{1,0:T(8,128)(2,1)S(1)}, u32[]{:S(2)}, u32[]{:S(2)}) collective-permute-start(bf16[256,256]{1,0:T(8,128)(2,1)S(1)} %get-tuple-element.34), channel_id=1, source_target_pairs={{0,121},{1,122},{2,123},{3,124},{4,125},{5,126},{6,127},{7,120},{8... | collective-permute-start | bytes 393224 | tf_op jit(solution)/shard_map/ppermute | solution.py:250
  11.6 1.2 %collective-permute-start.2 = (bf16[256,256]{1,0:T(8,128)(2,1)S(1)}, bf16[256,256]{1,0:T(8,128)(2,1)S(1)}, u32[]{:S(2)}, u32[]{:S(2)}) collective-permute-start(bf16[256,256]{1,0:T(8,128)(2,1)S(1)} %get-tuple-element.39), channel_id=1, source_target_pairs={{0,121},{1,122},{2,123},{3,124},{4,125},{5,126},{6,127},{7,120},{8... | collective-permute-start | bytes 393224 | tf_op jit(solution)/shard_map/ppermute | solution.py:251
  12.8 1.8 %shard_map.96 = (f32[2048,256]{1,0:T(8,128)S(1)}, bf16[32,16,128]{2,1,0:T(8,128)(2,1)S(1)}, s32[16]{0:T(128)S(1)}) custom-call(f32[2048,256]{1,0:T(8,128)S(1)} %get-tuple-element.30.users, bf16[2048,256]{1,0:T(8,128)(2,1)S(1)} %get-tuple-element.31.resid, bf16[256,256]{1,0:T(8,128)(2,1)S(1)} %get-tuple-element.32.scaled, s32[16,1,2,16]{3,2,1,0:T(2,128)} %ids_u.3, ...), custom_call_target="tpu_custom_call" | custom-call | tf_op jit(solution)/shard_map/pallas_call | solution.py:198
  14.6 0.0 collective-permute-done.1.later
  14.6 0.6 %shard_map.97.dense = bf16[32,128,128]{2,1,0:T(8,128)(2,1)S(1)} custom-call(bf16[16,128,128]{2,1,0:T(8,128)(2,1)S(1)} %collective-permute-done.1.later, s32[16]{0:T(128)S(1)} %get-tuple-element.36.codes), custom_call_target="tpu_custom_call" | custom-call | tf_op jit(solution)/shard_map/pallas_call | solution.py:198
  15.2 2.1 %collective-permute-done.items = bf16[256,256]{1,0:T(8,128)(2,1)S(1)} collective-permute-done((bf16[256,256]{1,0:T(8,128)(2,1)S(1)}, bf16[256,256]{1,0:T(8,128)(2,1)S(1)}, u32[]{:S(2)}, u32[]{:S(2)}) %collective-permute-start) | collective-permute-done | bytes 131104 | tf_op jit(solution)/shard_map/ppermute | solution.py:250
  17.3 1.0 %shard_map.98 = (f32[2048,256]{1,0:T(8,128)S(1)}, f32[256,256]{1,0:T(8,128)S(1)}, bf16[256,256]{1,0:T(8,128)(2,1)S(1)}) custom-call(f32[2048,256]{1,0:T(8,128)S(1)} %get-tuple-element.33.users, bf16[256,256]{1,0:T(8,128)(2,1)S(1)} %collective-permute-done.items, bf16[32,128,128]{2,1,0:T(8,128)(2,1)S(1)} %shard_map.97.dense, ...), custom_call_target="tpu_custom_call" | custom-call | tf_op jit(solution)/shard_map/pallas_call | solution.py:198
  18.4 4.0 %collective-permute-done.2.accum = bf16[256,256]{1,0:T(8,128)(2,1)S(1)} collective-permute-done((bf16[256,256]{1,0:T(8,128)(2,1)S(1)}, bf16[256,256]{1,0:T(8,128)(2,1)S(1)}, u32[]{:S(2)}, u32[]{:S(2)}) %collective-permute-start.2) | collective-permute-done | bytes 131104 | tf_op jit(solution)/shard_map/ppermute | solution.py:251
  22.4 1.1 %shard_map.99 = (bf16[2048,256]{1,0:T(8,128)(2,1)S(1)}, bf16[256,256]{1,0:T(8,128)(2,1)S(1)}, bf16[256,256]{1,0:T(8,128)(2,1)S(1)}) custom-call(f32[2048,256]{1,0:T(8,128)S(1)} %get-tuple-element.38.users, bf16[256,256]{1,0:T(8,128)(2,1)S(1)} %collective-permute-done.items, bf16[256,256]{1,0:T(8,128)(2,1)S(1)} %collective-permute-done.2.accum, ...), custom_call_target="tpu_custom_call" | custom-call | tf_op jit(solution)/shard_map/pallas_call | solution.py:198
  23.5 0.1 collective-permute-start.4
  23.5 0.1 collective-permute-start.3
  23.6 1.8 %shard_map.100 = f32[2048,256]{1,0:T(8,128)} custom-call(f32[2048,256]{1,0:T(8,128)S(1)} %get-tuple-element.38.users, bf16[2048,256]{1,0:T(8,128)(2,1)S(1)} %get-tuple-element.41.resid, bf16[256,256]{1,0:T(8,128)(2,1)S(1)} %get-tuple-element.42.scaled), custom_call_target="tpu_custom_call" | custom-call | tf_op jit(solution)/shard_map/pallas_call | solution.py:198
  25.4 5.8 %collective-permute-done.4 = bf16[256,256]{1,0:T(8,128)(2,1)S(1)} collective-permute-done((bf16[256,256]{1,0:T(8,128)(2,1)S(1)}, bf16[256,256]{1,0:T(8,128)(2,1)S(1)}, u32[]{:S(2)}, u32[]{:S(2)}) %collective-permute-start.4) | collective-permute-done | bytes 131104 | tf_op jit(solution)/shard_map/ppermute | solution.py:277
  31.2 1.4 %collective-permute-done.3 = bf16[256,256]{1,0:T(8,128)(2,1)S(1)} collective-permute-done((bf16[256,256]{1,0:T(8,128)(2,1)S(1)}, bf16[256,256]{1,0:T(8,128)(2,1)S(1)}, u32[]{:S(2)}, u32[]{:S(2)}) %collective-permute-start.3) | collective-permute-done | bytes 131104 | tf_op jit(solution)/shard_map/ppermute | solution.py:269
  32.6 0.9 %fusion.2 = (f32[256,256]{1,0:T(8,128)}, f32[256,256]{1,0:T(8,128)}) fusion(f32[256,256]{1,0:T(8,128)S(1)} %get-tuple-element.43, bf16[256,256]{1,0:T(8,128)(2,1)S(1)} %collective-permute-done.3, bf16[256,256]{1,0:T(8,128)(2,1)S(1)} %collective-permute-done.4, f32[256,256]{1,0:T(8,128)S(1)} %get-tuple-element.45), kind=kLoop, calls=%fused_computation.6 | loop fusion | flops 917504 | bytes 1310720 | tf_op jit(solution)/shard_map/sub | solution.py:114
Async XLA Ops:
  2.7 11.8 %collective-permute-start.1 = (bf16[16,128,128]{2,1,0:T(8,128)(2,1)S(1)}, bf16[16,128,128]{2,1,0:T(8,128)(2,1)S(1)}, u32[]{:S(2)}, u32[]{:S(2)}) collective-permute-start(bf16[16,128,128]{2,1,0:T(8,128)(2,1)S(1)} %get-tuple-element.35), channel_id=1, source_target_pairs={{0,120},{8,0},{16,8},{24,16},{32,24},{40,32},{48,40},{56,48},{64,5... | collective-permute-start | bytes 1572872 | tf_op jit(solution)/shard_map/ppermute | solution.py:242
  8.7 8.6 %collective-permute-start = (bf16[256,256]{1,0:T(8,128)(2,1)S(1)}, bf16[256,256]{1,0:T(8,128)(2,1)S(1)}, u32[]{:S(2)}, u32[]{:S(2)}) collective-permute-start(bf16[256,256]{1,0:T(8,128)(2,1)S(1)} %get-tuple-element.34), channel_id=1, source_target_pairs={{0,121},{1,122},{2,123},{3,124},{4,125},{5,126},{6,127},{7,120},{8... | collective-permute-start | bytes 393224 | tf_op jit(solution)/shard_map/ppermute | solution.py:250
  11.6 10.8 %collective-permute-start.2 = (bf16[256,256]{1,0:T(8,128)(2,1)S(1)}, bf16[256,256]{1,0:T(8,128)(2,1)S(1)}, u32[]{:S(2)}, u32[]{:S(2)}) collective-permute-start(bf16[256,256]{1,0:T(8,128)(2,1)S(1)} %get-tuple-element.39), channel_id=1, source_target_pairs={{0,121},{1,122},{2,123},{3,124},{4,125},{5,126},{6,127},{7,120},{8... | collective-permute-start | bytes 393224 | tf_op jit(solution)/shard_map/ppermute | solution.py:251
  23.5 7.8 %collective-permute-start.4 = (bf16[256,256]{1,0:T(8,128)(2,1)S(1)}, bf16[256,256]{1,0:T(8,128)(2,1)S(1)}, u32[]{:S(2)}, u32[]{:S(2)}) collective-permute-start(bf16[256,256]{1,0:T(8,128)(2,1)S(1)} %get-tuple-element.46), channel_id=1, source_target_pairs={{121,0},{122,1},{123,2},{124,3},{125,4},{126,5},{127,6},{120,7},{1... | collective-permute-start | bytes 393224 | tf_op jit(solution)/shard_map/ppermute | solution.py:277
  23.5 9.1 %collective-permute-start.3 = (bf16[256,256]{1,0:T(8,128)(2,1)S(1)}, bf16[256,256]{1,0:T(8,128)(2,1)S(1)}, u32[]{:S(2)}, u32[]{:S(2)}) collective-permute-start(bf16[256,256]{1,0:T(8,128)(2,1)S(1)} %get-tuple-element.44), channel_id=1, source_target_pairs={{121,0},{122,1},{123,2},{124,3},{125,4},{126,5},{127,6},{120,7},{1... | collective-permute-start | bytes 393224 | tf_op jit(solution)/shard_map/ppermute | solution.py:269
